TPU v7x, 32 devices: a whole 2x2x4 slice. The times are simulated.
32 devices in a mesh: cells: 16 (over z, y, x), genes: 2 (over core).
Axes of the slice: x: 2, y: 2, z: 4, core: 2. Of those that a mesh axis runs over, the one named last changes fastest.
Arguments:
- expression: bfloat16 [16384, 4096], P('cells', 'genes'), may hold values from 0 to 3
- loading: bfloat16 [4096, 128], P('genes'), may hold values from -0.09375 to 0.09375
- kernel_width: bfloat16 [16384], P(('cells', 'genes')), may hold values from 10 to 20
- cluster: int32 [16384, 1], P(('cells', 'genes')), may hold values from 0 to 31, as said below
- quality: int32 [16384], P(('cells', 'genes')), may hold values from 0 to 1, as said below
Outputs:
- smoothed: float32 [16384, 128], P(('cells', 'genes'))
Inputs may be any that keep to these rules, and one draw needn't show every extreme that they name: Among the 512 cells of one device no cluster appears more than 32 times; one cluster appears exactly 32 times in every device, so that it holds 1024 cells; every cluster appears somewhere. All cells of a cluster that holds 1024 cells have quality 1.
All inputs are finite; a program needn't handle non-finite values.
Results may differ from a plain program's by a relative error of at most 0.0029.
Values may be sent and summed in bfloat16 or wider, within the bound.
No kernel may reach another device: no remote copies, remote signals or barrier semaphores. Data moves between devices by JAX's collectives and lax.ppermute only.
A program may use at most 64 MiB of HBM per device.

v0:
```python
import jax
import jax.numpy as jnp
from jax import lax
from jax.sharding import PartitionSpec as P


def diffuse(slot_rows, widths):
    widths = widths.astype(jnp.float32)
    present = (widths > 0).astype(jnp.float32)
    as_float = slot_rows.astype(jnp.float32)
    sq_norms = jnp.sum(as_float * as_float, axis=1)
    products = jnp.dot(slot_rows, slot_rows.T, preferred_element_type=jnp.float32)
    distance = sq_norms[:, None] + sq_norms[None, :] - 2.0 * products
    pair_live = present[:, None] * present[None, :]
    width_pair = jnp.where(
        pair_live > 0, widths[:, None] * widths[None, :], jnp.ones_like(pair_live)
    )
    affinity = jnp.exp(-distance / width_pair) * pair_live
    row_total = jnp.sum(affinity, axis=1) + (1.0 - present)
    weights = (affinity / row_total[:, None]).astype(jnp.bfloat16)
    one_step = 0.5 * (as_float + jnp.dot(weights, slot_rows, preferred_element_type=jnp.float32))
    two_steps = 0.5 * (
        one_step
        + jnp.dot(weights, one_step.astype(jnp.bfloat16), preferred_element_type=jnp.float32)
    )
    return two_steps


def body(expression, loading, kernel_width, cluster, quality):
    gene_count = lax.axis_size("genes")
    cell_count = lax.axis_size("cells")
    devices = gene_count * cell_count
    local_rows = kernel_width.shape[0]
    capacity = max(1, 2 * local_rows // devices)
    slot_count = devices * capacity
    comp_width = loading.shape[1]
    partial_sums = jnp.dot(expression, loading, preferred_element_type=jnp.float32)
    summed = lax.psum(partial_sums, "genes")
    row_start = lax.axis_index("genes") * local_rows
    embedded = lax.dynamic_slice_in_dim(summed, row_start, local_rows, 0)
    embedded = embedded.astype(jnp.bfloat16)
    is_live = quality == 1
    destination = cluster[:, 0]
    owner_cell = destination // gene_count
    owner_gene = destination % gene_count
    positions = jnp.arange(local_rows, dtype=jnp.int32)
    same_dest = (
        (destination[:, None] == destination[None, :])
        & is_live[None, :]
        & (positions[None, :] < positions[:, None])
    )
    slot_rank = jnp.sum(same_dest.astype(jnp.int32), axis=1)
    slot_index = jnp.where(
        is_live, (owner_gene * cell_count + owner_cell) * capacity + slot_rank, -1
    )
    onehot = (jnp.arange(slot_count, dtype=jnp.int32)[:, None] == slot_index[None, :]).astype(
        jnp.bfloat16
    )
    packed = jnp.dot(onehot, embedded, preferred_element_type=jnp.float32).astype(jnp.bfloat16)
    packed = packed.reshape(gene_count, cell_count, capacity, comp_width)
    packed_band = jnp.dot(onehot, kernel_width, preferred_element_type=jnp.float32).astype(
        jnp.bfloat16
    )
    packed_band = packed_band.reshape(gene_count, cell_count, capacity)
    arrived, arrived_band = (
        lax.all_to_all(
            lax.all_to_all(packed, "cells", split_axis=1, concat_axis=1, tiled=True),
            "genes",
            split_axis=0,
            concat_axis=0,
            tiled=True,
        ),
        lax.all_to_all(
            lax.all_to_all(packed_band, "cells", split_axis=1, concat_axis=1, tiled=True),
            "genes",
            split_axis=0,
            concat_axis=0,
            tiled=True,
        ),
    )
    smoothed = diffuse(arrived.reshape(slot_count, comp_width), arrived_band.reshape(slot_count))
    returned = lax.all_to_all(
        lax.all_to_all(
            smoothed.reshape(gene_count, cell_count, capacity, comp_width),
            "cells",
            split_axis=1,
            concat_axis=1,
            tiled=True,
        ),
        "genes",
        split_axis=0,
        concat_axis=0,
        tiled=True,
    )
    picked = jnp.take(returned.reshape(slot_count, comp_width), jnp.maximum(slot_index, 0), axis=0)
    return jnp.where(is_live[:, None], picked, embedded.astype(jnp.float32))


def solution(mesh):
    return jax.shard_map(
        body,
        mesh=mesh,
        in_specs=(
            P("cells", "genes"),
            P("genes", None),
            P(("cells", "genes")),
            P(("cells", "genes"), None),
            P(("cells", "genes")),
        ),
        out_specs=P(("cells", "genes"), None),
        check_vma=False,
    )
```

profile of v0, /device:TPU:0, one launch (start us, length us, event | category | flops | bytes accessed | tf_op | source)
XLA Modules:
  0.0 77.5 jit_solution(10935118953226406025)
XLA Ops:
  0.0 0.7 broadcast_compare_fusion.1
  0.7 1.0 %convert_reduce_fusion = s32[512]{0:T(512)S(1)} fusion(s32[512]{0:T(512)} %bitcast.19, pred[512]{0:T(512)(128)(4,1)S(1)} %broadcast_compare_fusion.1), kind=kLoop, calls=%fused_computation.14 | loop fusion | flops 1572352 | bytes 4608 | tf_op jit(solution)/shard_map/reduce_sum | solution.py:52
  1.8 0.7 broadcast_compare_fusion
  2.5 0.7 reshape.74
  3.2 0.5 fusion
  3.6 0.1 reshape.61
  3.7 0.6 copy.35
  4.3 8.3 %all-to-all-start.2 = ((bf16[2,16,32]{2,0,1:T(2,128)(2,1)}), bf16[2,16,32]{2,0,1:T(2,128)(2,1)S(1)}, u32[]{:S(2)}, u32[]{:S(2)}) async-start(bf16[2,16,32]{2,0,1:T(2,128)(2,1)} %copy.35), calls=%async_computation.2 | async-start | bytes 16384 | tf_op jit(solution)/shard_map/all_to_all | solution.py:74
  12.7 3.4 %fusion.19 = f32[1024,128]{1,0:T(8,128)S(1)} fusion(bf16[1024,2048]{1,0:T(8,128)(2,1)} %param.5, bf16[2048,128]{1,0:T(8,128)(2,1)S(1)} %copy-done), kind=kOutput, calls=%fused_computation.42 | convolution fusion | flops 536870912 | bytes 5242880 | tf_op jit(solution)/shard_map/dot_general | solution.py:37
  16.1 4.8 %all-reduce.1 = bf16[1024,128]{1,0:T(8,128)(2,1)S(1)} all-reduce(f32[1024,128]{1,0:T(8,128)S(1)} %fusion.19), channel_id=1, replica_groups=mesh['cells'=16,'genes'=2] {'genes'}, use_global_device_ids=true, to_apply=%region_1.2 | all-reduce | flops 131072 | bytes 786432 | tf_op jit(solution)/shard_map/psum | solution.py:38
  21.0 0.5 fusion.4
  21.4 0.7 copy.31
  22.2 0.0 all-to-all-done.2
  22.2 0.1 reshape.76
  22.3 3.7 %all_to_all.30 = bf16[2,2,256]{2,1,0:T(2,128)(2,1)S(1)} all-to-all(bf16[2,2,256]{2,1,0:T(2,128)(2,1)S(1)} %reshape.76), channel_id=1, replica_groups=mesh['cells'=16,'genes'=2] {'genes'}, dimensions={0} | all-to-all | bytes 4096 | tf_op jit(solution)/shard_map/all_to_all | solution.py:73
  25.9 6.9 %all-to-all-start = ((bf16[2,16,32,128]{3,2,0,1:T(8,128)(2,1)}), bf16[2,16,32,128]{3,2,0,1:T(8,128)(2,1)S(1)}, u32[]{:S(2)}, u32[]{:S(2)}) async-start(bf16[2,16,32,128]{3,2,0,1:T(8,128)(2,1)} %copy.31), calls=%async_computation | async-start | bytes 524288 | tf_op jit(solution)/shard_map/all_to_all | solution.py:67
  32.9 0.1 reshape.77
  32.9 0.1 reshape.64
  33.0 10.0 %all-to-all-done = bf16[2,16,32,128]{3,2,0,1:T(8,128)(2,1)S(1)} async-done(((bf16[2,16,32,128]{3,2,0,1:T(8,128)(2,1)}), bf16[2,16,32,128]{3,2,0,1:T(8,128)(2,1)S(1)}, u32[]{:S(2)}, u32[]{:S(2)}) %all-to-all-start) | async-done | bytes 262176 | tf_op jit(solution)/shard_map/all_to_all | solution.py:67
  43.1 3.9 %all_to_all.31 = bf16[2,16,32,128]{3,2,1,0:T(8,128)(2,1)S(1)} all-to-all(bf16[2,16,32,128]{3,2,1,0:T(8,128)(2,1)S(1)} %copy.32), channel_id=1, replica_groups=mesh['cells'=16,'genes'=2] {'genes'}, dimensions={0} | all-to-all | bytes 524288 | tf_op jit(solution)/shard_map/all_to_all | solution.py:66
  47.0 0.2 multiply_reduce_fusion
  47.2 0.1 add.54
  47.3 2.1 %fusion.18 = (f32[1024]{0:T(1024)S(1)}, f32[1024,1024]{0,1:T(8,128)S(1)}) fusion(f32[1024]{0:T(1024)S(1)} %reshape.64, f32[1024]{0:T(1024)S(1)} %compare_convert_fusion, bf16[1024,128]{1,0:T(8,128)(2,1)S(1)} %bitcast.16, f32[1024]{0:T(1024)S(1)} %add.54), kind=kOutput, calls=%fused_computation.41 | convolution fusion | flops 279968768 | bytes 4472832 | tf_op jit(solution)/shard_map/dot_general | solution.py:12
  49.4 0.6 divide_convert_fusion
  50.0 0.7 fusion.3
  50.8 0.8 fusion.2
  51.5 0.8 %copy.37 = f32[2,16,32,128]{3,2,0,1:T(8,128)} copy(f32[2,16,32,128]{3,2,1,0:T(8,128)S(1)} %bitcast.15) | data formatting | bytes 1048576 | tf_op jit(solution)/shard_map/reshape | solution.py:84
  52.4 3.6 %all-to-all-start.4 = ((f32[2,16,32,128]{3,2,0,1:T(8,128)}), f32[2,16,32,128]{3,2,0,1:T(8,128)S(1)}, u32[]{:S(2)}, u32[]{:S(2)}) async-start(f32[2,16,32,128]{3,2,0,1:T(8,128)} %copy.37), calls=%async_computation.4 | async-start | bytes 1048576 | tf_op jit(solution)/shard_map/all_to_all | solution.py:83
  56.0 15.4 %all-to-all-done.4 = f32[2,16,32,128]{3,2,0,1:T(8,128)S(1)} async-done(((f32[2,16,32,128]{3,2,0,1:T(8,128)}), f32[2,16,32,128]{3,2,0,1:T(8,128)S(1)}, u32[]{:S(2)}, u32[]{:S(2)}) %all-to-all-start.4) | async-done | bytes 524320 | tf_op jit(solution)/shard_map/all_to_all | solution.py:83
  71.4 4.2 %all_to_all.32 = f32[2,16,32,128]{3,2,1,0:T(8,128)S(1)} all-to-all(f32[2,16,32,128]{3,2,1,0:T(8,128)S(1)} %copy.38), channel_id=1, replica_groups=mesh['cells'=16,'genes'=2] {'genes'}, dimensions={0} | all-to-all | bytes 1048576 | tf_op jit(solution)/shard_map/all_to_all | solution.py:82
  75.6 1.0 %gather_fusion = f32[512,128]{1,0:T(8,128)S(1)} fusion(f32[1024,128]{1,0:T(8,128)S(1)} %bitcast.14, s32[1024]{0:T(1024)S(1)} %pad_clamp_fusion), kind=kCustom, calls=%fused_computation | custom fusion | bytes 526336 | tf_op jit(solution)/shard_map/jit(_take)/gather | solution.py:95
  76.6 0.9 %convert_select_fusion = f32[512,128]{1,0:T(8,128)} fusion(f32[512,128]{1,0:T(8,128)S(1)} %gather_fusion, pred[512]{0:T(512)(128)(4,1)S(1)} %get-tuple-element.5, pred[512]{0:T(512)(128)(4,1)S(1)} %broadcast_compare_fusion.1, bf16[1024,128]{1,0:T(8,128)(2,1)S(1)} %all-reduce.1, s32[]{:T(128)S(6)} %select_n.36), kind=kLoop, calls=%fused_computation.18 | loop fusion | flops 196608 | bytes 656388 | tf_op jit(solution)/shard_map/jit(_where)/select_n | solution.py:96
  (10 shorter events, 0.1 us)
Async XLA Ops:
  0.0 12.7 %copy-start = (bf16[2048,128]{1,0:T(8,128)(2,1)S(1)}, bf16[2048,128]{1,0:T(8,128)(2,1)}, u32[]{:S(2)}) copy-start(bf16[2048,128]{1,0:T(8,128)(2,1)} %param.6) | copy-start | bytes 1572868
  4.3 17.8 %all-to-all-start.2 = ((bf16[2,16,32]{2,0,1:T(2,128)(2,1)}), bf16[2,16,32]{2,0,1:T(2,128)(2,1)S(1)}, u32[]{:S(2)}, u32[]{:S(2)}) async-start(bf16[2,16,32]{2,0,1:T(2,128)(2,1)} %copy.35), calls=%async_computation.2 | async-start | bytes 16384 | tf_op jit(solution)/shard_map/all_to_all | solution.py:74
  25.9 17.1 %all-to-all-start = ((bf16[2,16,32,128]{3,2,0,1:T(8,128)(2,1)}), bf16[2,16,32,128]{3,2,0,1:T(8,128)(2,1)S(1)}, u32[]{:S(2)}, u32[]{:S(2)}) async-start(bf16[2,16,32,128]{3,2,0,1:T(8,128)(2,1)} %copy.31), calls=%async_computation | async-start | bytes 524288 | tf_op jit(solution)/shard_map/all_to_all | solution.py:67
  52.4 19.0 %all-to-all-start.4 = ((f32[2,16,32,128]{3,2,0,1:T(8,128)}), f32[2,16,32,128]{3,2,0,1:T(8,128)S(1)}, u32[]{:S(2)}, u32[]{:S(2)}) async-start(f32[2,16,32,128]{3,2,0,1:T(8,128)} %copy.37), calls=%async_computation.4 | async-start | bytes 1048576 | tf_op jit(solution)/shard_map/all_to_all | solution.py:83
where the time goes:
time: 78.1 us; the launch traced here: 77.5 us
  waiting for transfers between devices  25.5 us (33%)
  starting transfers between devices  18.8 us (24%)
  blocking collectives  16.6 us (21%)
  matrix products  7.93 us (10%)
  local copies, waits for them, and re-layouts  4.35 us (6%)
  other arithmetic  4.24 us (5%)
    all_to_all x1, waiting for transfers between devices, body(): lax.all_to_all(smoothed.reshape(gene_count, cell_count, capacity, comp_wi...  15.4 us
    all_to_all x1, waiting for transfers between devices, body(): lax.all_to_all(packed, 'cells', split_axis=1, concat_axis=1, tiled=True)  10 us
    all_to_all x1, starting transfers between devices, body(): lax.all_to_all(packed_band, 'cells', split_axis=1, concat_axis=1, tiled=T...  8.34 us
    all_to_all x1, starting transfers between devices, body(): lax.all_to_all(packed, 'cells', split_axis=1, concat_axis=1, tiled=True)  6.91 us
    psum x1, blocking collectives, body(): summed = lax.psum(partial_sums, 'genes')  4.82 us
    all_to_all x1, blocking collectives, body(): lax.all_to_all(lax.all_to_all(smoothed.reshape(gene_count, cell_count, ca...  4.15 us
    all_to_all x1, blocking collectives, body(): lax.all_to_all(lax.all_to_all(packed, 'cells', split_axis=1, concat_axis=...  3.94 us
    all_to_all x1, blocking collectives, body(): lax.all_to_all(lax.all_to_all(packed_band, 'cells', split_axis=1, concat_...  3.69 us
  transfers between devices with their start and end apart: 3, of which 2 were waited for; matrix products, arithmetic and copies ran while one was open for 6% of the time, Pallas kernels for 0%

commit v1 on v0

v1 whole, which is shorter than its diff:
```python
import functools

import jax
import jax.numpy as jnp
from jax import lax
from jax.experimental import pallas as pl
from jax.experimental.pallas import tpu as pltpu
from jax.sharding import PartitionSpec as P

AXES = ("cells", "genes")
LANES = 128
LOG2E = 1.4426950408889634
FAR = 1e30
NT = (((1,), (1,)), ((), ()))
VMEM = pl.BlockSpec(memory_space=pltpu.VMEM)
SMEM = pl.BlockSpec(memory_space=pltpu.SMEM)
ANY = pl.BlockSpec(memory_space=pl.ANY)


def project_kernel(chunks, part_ref, x_ref, loading_ref, out_ref, buf, sems):
    rows = out_ref.shape[0] // chunks
    base = part_ref[0] * out_ref.shape[0]
    copies = []
    for k in range(chunks):
        start = pl.multiple_of(base + k * rows, rows)
        copies.append(
            pltpu.make_async_copy(x_ref.at[pl.ds(start, rows), :], buf.at[k], sems.at[k])
        )
        copies[-1].start()
    for k in range(chunks):
        copies[k].wait()
        out_ref[pl.ds(k * rows, rows), :] = jnp.dot(
            buf[k], loading_ref[...], preferred_element_type=jnp.float32
        )


def project(part, expression, loading, rows):
    genes, width = loading.shape
    chunks = 8
    return pl.pallas_call(
        functools.partial(project_kernel, chunks),
        out_shape=jax.ShapeDtypeStruct((rows, width), jnp.float32),
        in_specs=[SMEM, ANY, VMEM],
        out_specs=VMEM,
        scratch_shapes=[
            pltpu.VMEM((chunks, rows // chunks, genes), expression.dtype),
            pltpu.SemaphoreType.DMA((chunks,)),
        ],
        cost_estimate=pl.CostEstimate(
            flops=2 * rows * genes * width,
            bytes_accessed=2 * genes * (rows + width),
            transcendentals=0,
        ),
        name="project",
    )(part, expression, loading)


def iota(shape, axis):
    return lax.broadcasted_iota(jnp.int32, shape, axis)


def slots_of(cluster_row, quality_row, n_dest):
    cells = cluster_row.shape[1]
    member = (iota((n_dest, cells), 0) == cluster_row) & (quality_row == 1)
    ones = jnp.where(member, 1.0, 0.0)
    earlier = jnp.where(iota((cells, cells), 0) < iota((cells, cells), 1), 1.0, 0.0)
    before = jnp.dot(
        ones.astype(jnp.bfloat16), earlier.astype(jnp.bfloat16), preferred_element_type=jnp.float32
    )
    rank = jnp.sum(before * ones, axis=0, keepdims=True).astype(jnp.int32)
    return ones, rank


def pack_kernel(cap, cluster_ref, quality_ref, width_ref, *refs):
    *parts, packed_ref, embedded_ref, slot_ref = refs
    n_dest, stride, _ = packed_ref.shape
    cells = embedded_ref.shape[0]
    cluster_row = cluster_ref[...]
    quality_row = quality_ref[...]
    ones, rank = slots_of(cluster_row, quality_row, n_dest)
    live = quality_row == 1
    slot = jnp.where(live, cluster_row * cap + rank, -1)
    slot_ref[...] = jnp.broadcast_to(slot, slot_ref.shape)
    total = parts[0][...]
    for part in parts[1:]:
        total = total + part[...]
    embedded = total.astype(jnp.bfloat16)
    embedded_ref[...] = embedded
    place = jnp.where(live, cluster_row * stride + rank, -1)
    onehot = jnp.where(iota((n_dest * stride, cells), 0) == place, 1.0, 0.0).astype(jnp.bfloat16)
    rows = jnp.dot(onehot, embedded, preferred_element_type=jnp.float32)
    same_rank = jnp.where(lax.rem(iota((LANES, cells), 0), cap) == rank, 1.0, 0.0)
    owned = (ones * width_ref[...].astype(jnp.float32)).astype(jnp.bfloat16)
    widths = lax.dot_general(
        owned, same_rank.astype(jnp.bfloat16), NT, preferred_element_type=jnp.float32
    )
    rows = rows.reshape(packed_ref.shape)
    rows = jnp.where(iota(rows.shape, 1) >= cap, widths[:, None, :], rows)
    packed_ref[...] = rows.astype(jnp.bfloat16)


def diffuse_kernel(row_block, rows_ref, width_ref, out_ref, left, right, gain, affinity, step):
    slots = rows_ref.shape[0]
    sources = width_ref.shape[0]
    groups = slots // LANES
    per = sources // groups
    widths = width_ref[...].astype(jnp.float32).reshape(groups, per, LANES)
    mine = lax.div(iota(widths.shape, 2), LANES // per) == iota(widths.shape, 1)
    widths = jnp.sum(jnp.where(mine, widths, 0.0), axis=1)
    present = widths > 0
    inverse = jnp.where(present, 1.0 / jnp.where(present, widths, 1.0), 1.0)
    absent_col = jnp.transpose(jnp.where(present, 0.0, 1.0))
    gain_col = jnp.transpose(inverse * -LOG2E)
    lane = iota((LANES, LANES), 1)
    for g in range(groups):
        block = pl.ds(g * LANES, LANES)
        rows = rows_ref[block, :]
        wide = rows.astype(jnp.float32)
        norm = jnp.sum(wide * wide, axis=1, keepdims=True) + absent_col[:, g : g + 1] * FAR
        high = norm.astype(jnp.bfloat16).astype(jnp.float32)
        middle = (norm - high).astype(jnp.bfloat16).astype(jnp.float32)
        low = norm - high - middle
        one = jnp.ones_like(norm)
        split = jnp.where(lane == 0, high, jnp.where(lane == 1, middle, low))
        left[block, :LANES] = rows
        right[block, :LANES] = (wide * -2.0).astype(jnp.bfloat16)
        left[block, LANES:] = jnp.where(
            lane < 3, split, jnp.where(lane < 6, one, 0.0)
        ).astype(jnp.bfloat16)
        split = jnp.where(lane == 3, high, jnp.where(lane == 4, middle, low))
        right[block, LANES:] = jnp.where(
            lane < 3, one, jnp.where(lane < 6, split, 0.0)
        ).astype(jnp.bfloat16)
        gain[block, :] = jnp.broadcast_to(gain_col[:, g : g + 1], (LANES, LANES))
        step[block, :LANES] = rows
        step[block, LANES:] = jnp.ones((LANES, LANES), jnp.bfloat16)
    inverse_row = jnp.concatenate([inverse[g : g + 1, :] for g in range(groups)], axis=1)
    blocks = [pl.ds(b * row_block, row_block) for b in range(slots // row_block)]
    ones_steps, totals = [], []
    for block in blocks:
        distance = lax.dot_general(
            left[block, :], right[...], NT, preferred_element_type=jnp.float32
        )
        power = distance * gain[block, :1] * inverse_row
        weights = jnp.exp2(power).astype(jnp.bfloat16)
        affinity[block, :] = weights
        both = jnp.dot(weights, step[...], preferred_element_type=jnp.float32)
        total = both[:, LANES:]
        total = jnp.where(total > 0, total, 1.0)
        scale = 1.0 / total
        ones_steps.append(0.5 * (rows_ref[block, :].astype(jnp.float32) + both[:, :LANES] * scale))
        totals.append(scale)
    for block, one_step in zip(blocks, ones_steps):
        step[block, :LANES] = one_step.astype(jnp.bfloat16)
    for block, one_step, scale in zip(blocks, ones_steps, totals):
        again = jnp.dot(affinity[block, :], step[:, :LANES], preferred_element_type=jnp.float32)
        out_ref[block, :] = (0.5 * (one_step + again * scale)).astype(out_ref.dtype)


def diffuse(rows, widths):
    slots, width = rows.shape
    return pl.pallas_call(
        functools.partial(diffuse_kernel, 256),
        out_shape=jax.ShapeDtypeStruct((slots, width), jnp.bfloat16),
        in_specs=[VMEM] * 2,
        out_specs=VMEM,
        scratch_shapes=[
            pltpu.VMEM((slots, 2 * width), jnp.bfloat16),
            pltpu.VMEM((slots, 2 * width), jnp.bfloat16),
            pltpu.VMEM((slots, LANES), jnp.float32),
            pltpu.VMEM((slots, slots), jnp.bfloat16),
            pltpu.VMEM((slots, 2 * width), jnp.bfloat16),
        ],
        name="diffuse",
    )(rows, widths)


def pick_kernel(slot_ref, returned_ref, embedded_ref, out_ref):
    slot = jnp.transpose(slot_ref[...])[:, :1]
    shape = (slot.shape[0], returned_ref.shape[0])
    onehot = jnp.where(iota(shape, 1) == slot, 1.0, 0.0).astype(jnp.bfloat16)
    picked = jnp.dot(onehot, returned_ref[...], preferred_element_type=jnp.float32)
    out_ref[...] = jnp.where(slot >= 0, picked, embedded_ref[...].astype(jnp.float32))


def body(expression, loading, kernel_width, cluster, quality):
    gene_count = lax.axis_size("genes")
    devices = gene_count * lax.axis_size("cells")
    local = kernel_width.shape[0]
    cap = max(1, 2 * local // devices)
    stride = 8 * (cap // 8 + 1)
    width = loading.shape[1]
    me = lax.axis_index("genes")
    parts = []
    for shift in range(1, gene_count):
        part = lax.rem(me + shift, gene_count).reshape(1)
        ring = [(i, (i + shift) % gene_count) for i in range(gene_count)]
        parts.append(lax.ppermute(project(part, expression, loading, local), "genes", ring))
    parts.append(project(me.reshape(1), expression, loading, local))
    packed, embedded, slot = pl.pallas_call(
        functools.partial(pack_kernel, cap),
        out_shape=[
            jax.ShapeDtypeStruct((devices, stride, width), jnp.bfloat16),
            jax.ShapeDtypeStruct((local, width), jnp.bfloat16),
            jax.ShapeDtypeStruct((8, local), jnp.int32),
        ],
        in_specs=[VMEM] * (3 + len(parts)),
        out_specs=[VMEM] * 3,
        name="pack",
    )(
        cluster.reshape(1, local),
        quality.reshape(1, local),
        kernel_width.reshape(1, local),
        *parts,
    )
    arrived = lax.all_to_all(packed, AXES, split_axis=0, concat_axis=0, tiled=True)
    rows = arrived[:, :cap, :].reshape(devices * cap, width)
    smoothed = diffuse(rows, arrived[:, cap, :])
    returned = lax.all_to_all(
        smoothed.reshape(devices, cap, width), AXES, split_axis=0, concat_axis=0, tiled=True
    )
    return pl.pallas_call(
        pick_kernel,
        out_shape=jax.ShapeDtypeStruct((local, width), jnp.float32),
        in_specs=[VMEM] * 3,
        out_specs=VMEM,
        name="pick",
    )(slot, returned.reshape(devices * cap, width), embedded)


def solution(mesh):
    return jax.shard_map(
        body,
        mesh=mesh,
        in_specs=(
            P("cells", "genes"),
            P("genes", None),
            P(AXES),
            P(AXES, None),
            P(AXES),
        ),
        out_specs=P(AXES, None),
        check_vma=False,
    )
```

time: 78.1 us -> 55.2 us (0.71)
  waiting for transfers between devices: 25.5 us -> 0.01 us
  Pallas kernels: 0 us -> 18.7 us
  starting transfers between devices: 18.8 us -> 0.56 us
  blocking collectives: 16.6 us -> 32.8 us
  matrix products: 7.93 us -> 0 us
  other arithmetic: 4.24 us -> 0 us
  local copies, waits for them, and re-layouts: 4.35 us -> 2.62 us
    all_to_all x3 -> x0, waiting for transfers between devices: 25.5 us -> none  [the longest x1 15.4 us: body(): lax.all_to_all(smoothed.reshape(gene_count, cell_count, capacity, comp_wi...]
    all_to_all x3 -> x2, blocking collectives: 11.8 us -> 32.8 us  [the longest x1 19 us: body(): lax.all_to_all(packed, AXES, split_axis=0, concat_axis=0, tiled=True)]
    all_to_all x3 -> x0, starting transfers between devices: 18.8 us -> none  [the longest x1 8.34 us: body(): lax.all_to_all(packed_band, 'cells', split_axis=1, concat_axis=1, tiled=T...]
    pallas_call x0 -> x5, Pallas kernels: none -> 18.7 us  [the longest x2 9.1 us: project(): pl.pallas_call(functools.partial(project_kernel, chunks), out_shape=jax.S...]
    dot_general x6 -> x0, matrix products: 7.93 us -> none  [the longest x1 3.43 us: body(): jnp.dot(expression, loading, preferred_element_type=jnp.float32)]
    psum x1 -> x0, blocking collectives: 4.82 us -> none  [body(): summed = lax.psum(partial_sums, 'genes')]
    reshape x4 -> x1, local copies, waits for them, and re-layouts: 2.25 us -> 0.59 us  [body(): kernel_width.reshape(1, local)]
    reduce_sum x2 -> x0, other arithmetic: 1.23 us -> none  [the longest x1 1.02 us: body(): slot_rank = jnp.sum(same_dest.astype(jnp.int32), axis=1)]
  transfers between devices with their start and end apart: 3 -> 1, of which waited for: 2 -> 0; matrix products, arithmetic and copies ran while one was open for 6% -> 1% of each run, Pallas kernels for 0% -> 8%
where the time goes in v1:
time: 55.2 us; the launch traced here: 54.8 us
  blocking collectives  32.8 us (59%)
  Pallas kernels  18.7 us (34%)
  local copies, waits for them, and re-layouts  2.62 us (5%)
  starting transfers between devices  0.56 us (1%)
    all_to_all x1, blocking collectives, body(): lax.all_to_all(packed, AXES, split_axis=0, concat_axis=0, tiled=True)  19 us
    all_to_all x1, blocking collectives, body(): lax.all_to_all(smoothed.reshape(devices, cap, width), AXES, split_axis=0,...  13.9 us
    pallas_call x2, Pallas kernels, project(): pl.pallas_call(functools.partial(project_kernel, chunks), out_shape=jax.S...  9.1 us
    pallas_call x1, Pallas kernels, diffuse(): pl.pallas_call(functools.partial(diffuse_kernel, 256), out_shape=jax.Shap...  4.61 us
    pallas_call x1, Pallas kernels, body(): pl.pallas_call(functools.partial(pack_kernel, cap), out_shape=[jax.ShapeD...  2.56 us
    pallas_call x1, Pallas kernels, body(): pl.pallas_call(pick_kernel, out_shape=jax.ShapeDtypeStruct((local, width)...  2.44 us
    unnamed x5, local copies, waits for them, and re-layouts  1.3 us
  transfers between devices with their start and end apart: 1, of which 0 were waited for; matrix products, arithmetic and copies ran while one was open for 1% of the time, Pallas kernels for 8%

profile of v1, /device:TPU:0, one launch (start us, length us, event | category | flops | bytes accessed | tf_op | source)
XLA Modules:
  0.0 54.8 jit_solution(15505260346206795865)
XLA Ops:
  0.0 0.0 copy-start.1
  0.0 4.6 %project.2 = f32[512,128]{1,0:T(8,128)} custom-call(s32[1]{0:T(128)} %bitcast.2.part_ref, bf16[1024,2048]{1,0:T(8,128)(2,1)} %x_ref.3, bf16[2048,128]{1,0:T(8,128)(2,1)} %loading_ref.3), custom_call_target="tpu_custom_call" | custom-call | flops 268435456 | bytes 2621440 | tf_op jit(solution)/shard_map/project/pallas_call | solution.py:40
  4.6 0.6 %collective-permute-start = (f32[512,128]{1,0:T(8,128)}, f32[512,128]{1,0:T(8,128)S(1)}, u32[]{:S(2)}, u32[]{:S(2)}) collective-permute-start(f32[512,128]{1,0:T(8,128)} %project.2), channel_id=1, source_target_pairs={{0,1},{1,0},{2,3},{3,2},{4,5},{5,4},{6,7},{7,6},{8,9},{9,8},{10,11... | collective-permute-start | bytes 786440 | tf_op jit(solution)/shard_map/ppermute | solution.py:198
  5.1 0.0 copy-done.1
  5.1 0.6 %reshape.26.width_ref = bf16[1,512]{1,0:T(2,128)(2,1)} reshape(bf16[512]{0:T(512)(128)(2,1)S(1)} %copy-done.1) | data formatting | bytes 2048 | tf_op jit(solution)/shard_map/reshape | solution.py:213
  5.7 4.5 %project.3.refs_1_ = f32[512,128]{1,0:T(8,128)} custom-call(s32[1]{0:T(128)} %bitcast.3.part_ref, bf16[1024,2048]{1,0:T(8,128)(2,1)} %x_ref.3, bf16[2048,128]{1,0:T(8,128)(2,1)} %loading_ref.3), custom_call_target="tpu_custom_call" | custom-call | flops 268435456 | bytes 2621440 | tf_op jit(solution)/shard_map/project/pallas_call | solution.py:40
  10.3 0.0 collective-permute-done.refs_0_
  10.3 0.0 copy-start
  10.3 0.7 %copy-done = f32[512,128]{1,0:T(8,128)} copy-done((f32[512,128]{1,0:T(8,128)}, f32[512,128]{1,0:T(8,128)S(1)}, u32[]{:S(2)}) %copy-start) | copy-done | bytes 262168
  11.0 2.6 %pack.1 = (bf16[32,40,128]{2,1,0:T(8,128)(2,1)}, bf16[512,128]{1,0:T(8,128)(2,1)}, s32[8,512]{1,0:T(8,128)}) custom-call(s32[1,512]{1,0:T(1,128)} %bitcast.14, s32[1,512]{1,0:T(1,128)} %bitcast.15, bf16[1,512]{1,0:T(2,128)(2,1)} %reshape.26.width_ref, f32[512,128]{1,0:T(8,128)} %copy-done, f32[512,128]{1,0:T(8,128)} %project.3.refs_1_), custom_call_target="tpu_custom_call" | custom-call | tf_op jit(solution)/shard_map/pack/pallas_call | solution.py:200
  13.6 19.0 %all_to_all.10 = bf16[32,40,128]{2,1,0:T(8,128)(2,1)S(1)} all-to-all(bf16[32,40,128]{2,1,0:T(8,128)(2,1)} %get-tuple-element.9), channel_id=1, replica_groups=mesh['cells'=16,'genes'=2] {'cells','genes'}, dimensions={0} | all-to-all | bytes 655360 | tf_op jit(solution)/shard_map/all_to_all | solution.py:216
  32.6 0.6 %copy.12 = bf16[32,1,128]{2,0,1:T(8,128)(2,1)} copy(bf16[32,1,128]{2,1,0:T(2,128)(2,1)S(1)} %slice.9) | data formatting | bytes 16384
  33.2 0.7 %slice.8 = bf16[32,32,128]{2,1,0:T(8,128)(2,1)} slice(bf16[32,40,128]{2,1,0:T(8,128)(2,1)S(1)} %all_to_all.10), slice={[0:32], [0:32], [0:128]} | slice | bytes 524288 | tf_op jit(solution)/shard_map/slice | solution.py:217
  33.9 4.6 %diffuse.1 = bf16[1024,128]{1,0:T(8,128)(2,1)} custom-call(bf16[1024,128]{1,0:T(8,128)(2,1)} %bitcast.10, bf16[32,128]{1,0:T(8,128)(2,1)} %bitcast.13), custom_call_target="tpu_custom_call" | custom-call | tf_op jit(solution)/shard_map/diffuse/pallas_call | solution.py:162
  38.5 13.9 %all_to_all.11 = bf16[32,32,128]{2,1,0:T(8,128)(2,1)} all-to-all(bf16[32,32,128]{2,1,0:T(8,128)(2,1)} %bitcast.11), channel_id=1, replica_groups=mesh['cells'=16,'genes'=2] {'cells','genes'}, dimensions={0} | all-to-all | bytes 524288 | tf_op jit(solution)/shard_map/all_to_all | solution.py:219
  52.3 2.4 %pick.1 = f32[512,128]{1,0:T(8,128)} custom-call(s32[8,512]{1,0:T(8,128)} %get-tuple-element.8.slot_ref, bf16[1024,128]{1,0:T(8,128)(2,1)} %bitcast.12, bf16[512,128]{1,0:T(8,128)(2,1)} %get-tuple-element.10.embedded_ref), custom_call_target="tpu_custom_call" | custom-call | tf_op jit(solution)/shard_map/pick/pallas_call | solution.py:222
  (1 shorter events, 0.0 us)
Async XLA Ops:
  0.0 5.1 %copy-start.1 = (bf16[512]{0:T(512)(128)(2,1)S(1)}, bf16[512]{0:T(512)(128)(2,1)}, u32[]{:S(2)}) copy-start(bf16[512]{0:T(512)(128)(2,1)} %param.7) | copy-start | bytes 3076
  4.6 5.7 %collective-permute-start = (f32[512,128]{1,0:T(8,128)}, f32[512,128]{1,0:T(8,128)S(1)}, u32[]{:S(2)}, u32[]{:S(2)}) collective-permute-start(f32[512,128]{1,0:T(8,128)} %project.2), channel_id=1, source_target_pairs={{0,1},{1,0},{2,3},{3,2},{4,5},{5,4},{6,7},{7,6},{8,9},{9,8},{10,11... | collective-permute-start | bytes 786440 | tf_op jit(solution)/shard_map/ppermute | solution.py:198
  10.3 0.7 %copy-start = (f32[512,128]{1,0:T(8,128)}, f32[512,128]{1,0:T(8,128)S(1)}, u32[]{:S(2)}) copy-start(f32[512,128]{1,0:T(8,128)S(1)} %collective-permute-done.refs_0_) | copy-start | bytes 786436

commit v2 on v1

v2 whole, which is shorter than its diff:
```python
import functools

import jax
import jax.numpy as jnp
from jax import lax
from jax.experimental import pallas as pl
from jax.experimental.pallas import tpu as pltpu
from jax.sharding import PartitionSpec as P

AXES = ("cells", "genes")
LANES = 128
LOG2E = 1.4426950408889634
FAR = 1e30
NT = (((1,), (1,)), ((), ()))
VMEM = pl.BlockSpec(memory_space=pltpu.VMEM)
HBM = pl.BlockSpec(memory_space=pltpu.HBM)
CHUNKS = 1


def grant(mebibytes):
    return pltpu.CompilerParams(vmem_limit_bytes=mebibytes << 20)


def iota(shape, axis):
    return lax.broadcasted_iota(jnp.int32, shape, axis)


def ranks(cluster_row, live, clusters):
    cells = cluster_row.shape[1]
    member = jnp.where((iota((clusters, cells), 0) == cluster_row) & live, 1.0, 0.0)
    earlier = jnp.where(iota((cells, cells), 0) < iota((cells, cells), 1), 1.0, 0.0)
    before = jnp.dot(
        member.astype(jnp.bfloat16),
        earlier.astype(jnp.bfloat16),
        preferred_element_type=jnp.float32,
    )
    return jnp.sum(before * member, axis=0, keepdims=True).astype(jnp.int32)


def project_kernel(stride, x_ref, loading_ref, cluster_ref, quality_ref, *refs):
    own_ref, weights_ref, place_ref, rank_ref, *out_refs, x_buf, labels, sems = refs
    parts = len(out_refs) + 1
    rows = own_ref.shape[0]
    depth = rows // CHUNKS
    me = lax.axis_index("genes")
    small = [
        pltpu.make_async_copy(cluster_ref, labels.at[0], sems.at[0, CHUNKS]),
        pltpu.make_async_copy(quality_ref, labels.at[1], sems.at[1, CHUNKS]),
    ]
    weights = pltpu.make_async_copy(loading_ref, weights_ref, sems.at[parts, CHUNKS])
    for copy in [*small, weights]:
        copy.start()
    copies = []
    for p in range(parts):
        buffer = own_ref if p == parts - 1 else x_buf.at[p]
        first = lax.rem(me + p + 1, parts) * rows
        copies.append([])
        for c in range(CHUNKS):
            source = x_ref.at[pl.ds(pl.multiple_of(first + c * depth, depth), depth), :]
            target = buffer.at[pl.ds(c * depth, depth), :]
            copies[p].append(pltpu.make_async_copy(source, target, sems.at[p, c]))
            copies[p][c].start()
    for copy in small:
        copy.wait()
    cluster_row = labels[0]
    live = labels[1] == 1
    rank = ranks(cluster_row, live, place_ref.shape[0] // stride)
    rank_ref[...] = jnp.broadcast_to(rank, rank_ref.shape)
    place = jnp.where(live, cluster_row * stride + rank, -1)
    place_ref[...] = jnp.where(iota(place_ref.shape, 0) == place, 1.0, 0.0).astype(jnp.bfloat16)
    weights.wait()
    for p in range(parts):
        for copy in copies[p]:
            copy.wait()
        if p < parts - 1:
            out_refs[p][...] = jnp.dot(
                x_buf[p], weights_ref[...], preferred_element_type=jnp.float32
            )


def project(expression, loading, cluster, quality, parts, devices, stride):
    cells, genes = expression.shape
    width = loading.shape[1]
    rows = cells // parts
    others = parts - 1
    operands = (expression, loading, cluster.reshape(1, rows), quality.reshape(1, rows))
    return pl.pallas_call(
        functools.partial(project_kernel, stride),
        out_shape=[
            jax.ShapeDtypeStruct((rows, genes), expression.dtype),
            jax.ShapeDtypeStruct((genes, width), loading.dtype),
            jax.ShapeDtypeStruct((devices * stride, rows), jnp.bfloat16),
            jax.ShapeDtypeStruct((8, rows), jnp.int32),
        ]
        + [jax.ShapeDtypeStruct((rows, width), jnp.float32)] * others,
        in_specs=[HBM] * 4,
        out_specs=[VMEM] * (4 + others),
        scratch_shapes=[
            pltpu.VMEM((max(others, 1), rows, genes), expression.dtype),
            pltpu.VMEM((2, 1, rows), jnp.int32),
            pltpu.SemaphoreType.DMA((parts + 1, CHUNKS + 1)),
        ],
        compiler_params=grant(24),
        name="project",
    )(*[pltpu.with_memory_space_constraint(operand, pltpu.HBM) for operand in operands])


def project_own_kernel(cap, x_ref, weights_ref, cluster_ref, quality_ref, rank_ref, width_ref, *refs):
    out_ref, spare_ref, pick_ref = refs
    out_ref[...] = jnp.dot(x_ref[...], weights_ref[...], preferred_element_type=jnp.float32)
    cells = x_ref.shape[0]
    live = quality_ref[...] == 1
    widths = jnp.where(live, width_ref[...].astype(jnp.float32), 0.0)
    rank = rank_ref[:1, :]
    slot = jnp.where(live, cluster_ref[...] * cap + rank, -1)
    slot = jnp.transpose(jnp.broadcast_to(slot, (8, cells)))[:, :1]
    pick_ref[...] = jnp.where(iota(pick_ref.shape, 1) == slot, 1.0, 0.0).astype(jnp.bfloat16)
    member = iota((spare_ref.shape[0], cells), 0) == cluster_ref[...]
    owned = jnp.where(member, widths, 0.0).astype(jnp.bfloat16)
    same_rank = jnp.where(lax.rem(iota((LANES, cells), 0), cap) == rank, 1.0, 0.0)
    spare_ref[...] = lax.dot_general(
        owned, same_rank.astype(jnp.bfloat16), NT, preferred_element_type=jnp.float32
    )


def project_own(own, weights, cluster, quality, rank, kernel_width, devices, cap):
    rows, genes = own.shape
    width = weights.shape[1]
    return pl.pallas_call(
        functools.partial(project_own_kernel, cap),
        out_shape=[
            jax.ShapeDtypeStruct((rows, width), jnp.float32),
            jax.ShapeDtypeStruct((devices, LANES), jnp.float32),
            jax.ShapeDtypeStruct((rows, devices * cap), jnp.bfloat16),
        ],
        in_specs=[VMEM] * 6,
        out_specs=[VMEM] * 3,
        cost_estimate=pl.CostEstimate(
            flops=2 * rows * genes * width,
            bytes_accessed=2 * genes * (rows + width),
            transcendentals=0,
        ),
        compiler_params=grant(10),
        name="project_own",
    )(
        own,
        weights,
        cluster.reshape(1, rows),
        quality.reshape(1, rows),
        rank,
        kernel_width.reshape(1, rows),
    )


def pack_kernel(cap, place_ref, spare_ref, *refs):
    *parts, packed_ref, embedded_ref = refs
    total = parts[0][...]
    for part in parts[1:]:
        total = total + part[...]
    embedded = total.astype(jnp.bfloat16)
    embedded_ref[...] = embedded
    rows = jnp.dot(place_ref[...], embedded, preferred_element_type=jnp.float32)
    rows = rows.reshape(packed_ref.shape)
    rows = jnp.where(iota(rows.shape, 1) >= cap, spare_ref[...][:, None, :], rows)
    packed_ref[...] = rows.astype(jnp.bfloat16)


def pack(parts, place, spare, cap, stride):
    cells, width = parts[0].shape
    return pl.pallas_call(
        functools.partial(pack_kernel, cap),
        out_shape=[
            jax.ShapeDtypeStruct((spare.shape[0], stride, width), jnp.bfloat16),
            jax.ShapeDtypeStruct((cells, width), jnp.bfloat16),
        ],
        in_specs=[VMEM] * (2 + len(parts)),
        out_specs=[VMEM] * 2,
        compiler_params=grant(10),
        name="pack",
    )(place, spare, *parts)


def diffuse_kernel(row_block, cap, arrived_ref, out_ref, left, right, gain, affinity, step):
    sources = arrived_ref.shape[0]
    slots = out_ref.shape[0]
    groups = slots // LANES
    per = LANES // cap
    widths = arrived_ref[:, cap, :].astype(jnp.float32).reshape(groups, per, LANES)
    mine = lax.div(iota(widths.shape, 2), LANES // per) == iota(widths.shape, 1)
    widths = jnp.sum(jnp.where(mine, widths, 0.0), axis=1)
    present = widths > 0
    inverse = jnp.where(present, 1.0 / jnp.where(present, widths, 1.0), 1.0)
    absent_col = jnp.transpose(jnp.where(present, 0.0, 1.0))
    gain_col = jnp.transpose(inverse * -LOG2E)
    lane = iota((LANES, LANES), 1)
    for g in range(groups):
        block = pl.ds(g * LANES, LANES)
        rows = jnp.concatenate(
            [arrived_ref[s, :cap, :] for s in range(g * per, (g + 1) * per)], axis=0
        )
        wide = rows.astype(jnp.float32)
        norm = jnp.sum(wide * wide, axis=1, keepdims=True) + absent_col[:, g : g + 1] * FAR
        high = norm.astype(jnp.bfloat16).astype(jnp.float32)
        middle = (norm - high).astype(jnp.bfloat16).astype(jnp.float32)
        low = norm - high - middle
        one = jnp.ones_like(norm)
        split = jnp.where(lane == 0, high, jnp.where(lane == 1, middle, low))
        left[block, :LANES] = rows
        right[block, :LANES] = (wide * -2.0).astype(jnp.bfloat16)
        left[block, LANES:] = jnp.where(
            lane < 3, split, jnp.where(lane < 6, one, 0.0)
        ).astype(jnp.bfloat16)
        split = jnp.where(lane == 3, high, jnp.where(lane == 4, middle, low))
        right[block, LANES:] = jnp.where(
            lane < 3, one, jnp.where(lane < 6, split, 0.0)
        ).astype(jnp.bfloat16)
        gain[block, :] = jnp.broadcast_to(gain_col[:, g : g + 1], (LANES, LANES))
        step[block, :LANES] = rows
        step[block, LANES:] = jnp.ones((LANES, LANES), jnp.bfloat16)
    inverse_row = jnp.concatenate([inverse[g : g + 1, :] for g in range(groups)], axis=1)
    blocks = [pl.ds(b * row_block, row_block) for b in range(slots // row_block)]
    ones_steps, totals = [], []
    for block in blocks:
        distance = lax.dot_general(
            left[block, :], right[...], NT, preferred_element_type=jnp.float32
        )
        power = distance * gain[block, :1] * inverse_row
        weights = jnp.exp2(power).astype(jnp.bfloat16)
        affinity[block, :] = weights
        both = jnp.dot(weights, step[...], preferred_element_type=jnp.float32)
        total = both[:, LANES:]
        total = jnp.where(total > 0, total, 1.0)
        scale = 1.0 / total
        ones_steps.append(0.5 * (left[block, :LANES].astype(jnp.float32) + both[:, :LANES] * scale))
        totals.append(scale)
    for block, one_step in zip(blocks, ones_steps):
        step[block, :LANES] = one_step.astype(jnp.bfloat16)
    for block, one_step, scale in zip(blocks, ones_steps, totals):
        again = jnp.dot(affinity[block, :], step[:, :LANES], preferred_element_type=jnp.float32)
        out_ref[block, :] = (0.5 * (one_step + again * scale)).astype(out_ref.dtype)


def diffuse(arrived, cap):
    sources, _, width = arrived.shape
    slots = sources * cap
    return pl.pallas_call(
        functools.partial(diffuse_kernel, 256, cap),
        out_shape=jax.ShapeDtypeStruct((slots, width), jnp.bfloat16),
        in_specs=[VMEM],
        out_specs=VMEM,
        scratch_shapes=[
            pltpu.VMEM((slots, 2 * width), jnp.bfloat16),
            pltpu.VMEM((slots, 2 * width), jnp.bfloat16),
            pltpu.VMEM((slots, LANES), jnp.float32),
            pltpu.VMEM((slots, slots), jnp.bfloat16),
            pltpu.VMEM((slots, 2 * width), jnp.bfloat16),
        ],
        compiler_params=grant(16),
        name="diffuse",
    )(arrived)


def pick_kernel(quality_ref, pick_ref, returned_ref, embedded_ref, out_ref):
    picked = jnp.dot(pick_ref[...], returned_ref[...], preferred_element_type=jnp.float32)
    live = jnp.transpose(jnp.broadcast_to(quality_ref[...], (8, out_ref.shape[0])))[:, :1] == 1
    out_ref[...] = jnp.where(live, picked, embedded_ref[...].astype(jnp.float32))


def pick(quality, pick_onehot, returned, embedded):
    cells, width = embedded.shape
    return pl.pallas_call(
        pick_kernel,
        out_shape=jax.ShapeDtypeStruct((cells, width), jnp.float32),
        in_specs=[VMEM] * 4,
        out_specs=VMEM,
        compiler_params=grant(8),
        name="pick",
    )(quality.reshape(1, cells), pick_onehot, returned, embedded)


def body(expression, loading, kernel_width, cluster, quality):
    gene_count = lax.axis_size("genes")
    devices = gene_count * lax.axis_size("cells")
    cap = max(1, 2 * kernel_width.shape[0] // devices)
    stride = 8 * (cap // 8 + 1)
    width = loading.shape[1]
    own, weights, place, rank, *partials = project(
        expression, loading, cluster, quality, gene_count, devices, stride
    )
    parts = []
    for shift, partial in enumerate(partials, 1):
        ring = [(i, (i + shift) % gene_count) for i in range(gene_count)]
        parts.append(lax.ppermute(partial, "genes", ring))
    own_part, spare, pick_onehot = project_own(
        own, weights, cluster, quality, rank, kernel_width, devices, cap
    )
    parts.append(own_part)
    packed, embedded = pack(parts, place, spare, cap, stride)
    arrived = lax.all_to_all(packed, AXES, split_axis=0, concat_axis=0, tiled=True)
    smoothed = diffuse(arrived, cap)
    returned = lax.all_to_all(
        smoothed.reshape(devices, cap, width), AXES, split_axis=0, concat_axis=0, tiled=True
    )
    return pick(quality, pick_onehot, returned.reshape(devices * cap, width), embedded)


def solution(mesh):
    return jax.shard_map(
        body,
        mesh=mesh,
        in_specs=(
            P("cells", "genes"),
            P("genes", None),
            P(AXES),
            P(AXES, None),
            P(AXES),
        ),
        out_specs=P(AXES, None),
        check_vma=False,
    )
```

time: 55.2 us -> 41 us (0.74)
  Pallas kernels: 18.7 us -> 8.12 us
  local copies, waits for them, and re-layouts: 2.62 us -> 0.02 us
  blocking collectives: 32.8 us -> 31.8 us
    pallas_call x5, Pallas kernels: 18.7 us -> 8.12 us  [the longest x1 2.96 us: diffuse(): pl.pallas_call(functools.partial(diffuse_kernel, 256, cap), out_shape=jax...]
    unnamed x5 -> x6, local copies, waits for them, and re-layouts: 1.3 us -> 0.01 us
    all_to_all x1, blocking collectives: 13.9 us -> 12.7 us  [body(): lax.all_to_all(smoothed.reshape(devices, cap, width), AXES, split_axis=0,...]
    slice x2 -> x0, local copies, waits for them, and re-layouts: 0.73 us -> none  [the longest x1 0.72 us: body(): rows = arrived[:, :cap, :].reshape(devices * cap, width)]
    reshape x1, local copies, waits for them, and re-layouts: 0.59 us -> 0.01 us  [project_own(): kernel_width.reshape(1, rows)]
  transfers between devices with their start and end apart: 1 -> 1, of which waited for: 0 -> 1; matrix products, arithmetic and copies ran while one was open for 1% -> 0% of each run, Pallas kernels for 8% -> 2%
where the time goes in v2:
time: 41 us; the launch traced here: 40.8 us
  blocking collectives  31.8 us (78%)
  Pallas kernels  8.12 us (20%)
  starting transfers between devices  0.56 us (1%)
    all_to_all x1, blocking collectives, body(): lax.all_to_all(packed, AXES, split_axis=0, concat_axis=0, tiled=True)  19.1 us
    all_to_all x1, blocking collectives, body(): lax.all_to_all(smoothed.reshape(devices, cap, width), AXES, split_axis=0,...  12.7 us
    pallas_call x1, Pallas kernels, diffuse(): pl.pallas_call(functools.partial(diffuse_kernel, 256, cap), out_shape=jax...  2.96 us
    pallas_call x1, Pallas kernels, project(): pl.pallas_call(functools.partial(project_kernel, stride), out_shape=[jax....  2.6 us
    pallas_call x1, Pallas kernels, pick(): pl.pallas_call(pick_kernel, out_shape=jax.ShapeDtypeStruct((cells, width)...  1.22 us
    pallas_call x1, Pallas kernels, project_own(): pl.pallas_call(functools.partial(project_own_kernel, cap), out_shape=[jax...  0.84 us
  transfers between devices with their start and end apart: 1, of which 1 were waited for; matrix products, arithmetic and copies ran while one was open for 0% of the time, Pallas kernels for 2%

profile of v2, /device:TPU:0, one launch (start us, length us, event | category | flops | bytes accessed | tf_op | source)
XLA Modules:
  0.0 40.8 jit_solution(5793308294721408780)
XLA Ops:
  0.0 0.0 copy-start.2
  0.0 0.0 copy-start
  0.0 0.0 copy-start.1
  0.0 2.6 %project.1 = (bf16[512,2048]{1,0:T(8,128)(2,1)S(1)}, bf16[2048,128]{1,0:T(8,128)(2,1)S(1)}, bf16[1280,512]{1,0:T(8,128)(2,1)S(1)}, s32[8,512]{1,0:T(8,128)S(1)}, f32[512,128]{1,0:T(8,128)S(1)}) custom-call(bf16[1024,2048]{1,0:T(8,128)(2,1)} %x_ref.1, bf16[2048,128]{1,0:T(8,128)(2,1)} %loading_ref.1, s32[1,512]{1,0:T(1,128)} %bitcast.9, s32[1,512]{1,0:T(1,128)} %bitcast.6), custom_call_target="tpu_custom_call" | custom-call | tf_op jit(solution)/shard_map/project/pallas_call | solution.py:87
  2.6 0.6 %collective-permute-start = (f32[512,128]{1,0:T(8,128)S(1)}, f32[512,128]{1,0:T(8,128)S(1)}, u32[]{:S(2)}, u32[]{:S(2)}) collective-permute-start(f32[512,128]{1,0:T(8,128)S(1)} %get-tuple-element.21), channel_id=1, source_target_pairs={{0,1},{1,0},{2,3},{3,2},{4,5},{5,4},{6,7},{7,6},{8,9},{9,8},{10,11... | collective-permute-start | bytes 786440 | tf_op jit(solution)/shard_map/ppermute | solution.py:293
  3.2 0.0 copy-done.2
  3.2 0.0 copy-done
  3.2 0.0 copy-done.1
  3.2 0.8 %project_own.1 = (f32[512,128]{1,0:T(8,128)S(1)}, f32[32,128]{1,0:T(8,128)S(1)}, bf16[512,1024]{1,0:T(8,128)(2,1)S(1)}) custom-call(bf16[512,2048]{1,0:T(8,128)(2,1)S(1)} %get-tuple-element.15.x_ref, bf16[2048,128]{1,0:T(8,128)(2,1)S(1)} %get-tuple-element.16.weights_ref, s32[1,512]{1,0:T(1,128)S(1)} %bitcast.10, s32[1,512]{1,0:T(1,128)S(1)} %bitcast.7, ...), custom_call_target="tpu_custom_call" | custom-call | flops 268435456 | bytes 2621440 | tf_op jit(solution)/shard_map/project_own/pallas_call | solution.py:129
  4.0 0.3 collective-permute-done.refs_0_
  4.3 0.5 %pack.1 = (bf16[32,40,128]{2,1,0:T(8,128)(2,1)S(1)}, bf16[512,128]{1,0:T(8,128)(2,1)S(1)}) custom-call(bf16[1280,512]{1,0:T(8,128)(2,1)S(1)} %get-tuple-element.19.place_ref, f32[32,128]{1,0:T(8,128)S(1)} %get-tuple-element.20.spare_ref, f32[512,128]{1,0:T(8,128)S(1)} %collective-permute-done.refs_0_, f32[512,128]{1,0:T(8,128)S(1)} %get-tuple-element.22.refs_1_), custom_call_target="tpu_custom_call" | custom-call | tf_op jit(solution)/shard_map/pack/pallas_call | solution.py:170
  4.8 19.1 %all_to_all.10.arrived_ref = bf16[32,40,128]{2,1,0:T(8,128)(2,1)S(1)} all-to-all(bf16[32,40,128]{2,1,0:T(8,128)(2,1)S(1)} %get-tuple-element.23), channel_id=1, replica_groups=mesh['cells'=16,'genes'=2] {'cells','genes'}, dimensions={0} | all-to-all | bytes 655360 | tf_op jit(solution)/shard_map/all_to_all | solution.py:299
  23.9 3.0 %diffuse.1 = bf16[1024,128]{1,0:T(8,128)(2,1)S(1)} custom-call(bf16[32,40,128]{2,1,0:T(8,128)(2,1)S(1)} %all_to_all.10.arrived_ref), custom_call_target="tpu_custom_call" | custom-call | tf_op jit(solution)/shard_map/diffuse/pallas_call | solution.py:246
  26.9 12.7 %all_to_all.11 = bf16[32,32,128]{2,1,0:T(8,128)(2,1)S(1)} all-to-all(bf16[32,32,128]{2,1,0:T(8,128)(2,1)S(1)} %bitcast.4), channel_id=1, replica_groups=mesh['cells'=16,'genes'=2] {'cells','genes'}, dimensions={0} | all-to-all | bytes 524288 | tf_op jit(solution)/shard_map/all_to_all | solution.py:301
  39.6 1.2 %pick.1 = f32[512,128]{1,0:T(8,128)} custom-call(s32[1,512]{1,0:T(1,128)S(1)} %bitcast.8, bf16[512,1024]{1,0:T(8,128)(2,1)S(1)} %get-tuple-element.18.pick_ref, bf16[1024,128]{1,0:T(8,128)(2,1)S(1)} %bitcast.5, bf16[512,128]{1,0:T(8,128)(2,1)S(1)} %get-tuple-element.24.embedded_ref), custom_call_target="tpu_custom_call" | custom-call | tf_op jit(solution)/shard_map/pick/pallas_call | solution.py:271
  (1 shorter events, 0.0 us)
Async XLA Ops:
  0.0 3.2 %copy-start.2 = (bf16[512]{0:T(512)(128)(2,1)S(1)}, bf16[512]{0:T(512)(128)(2,1)}, u32[]{:S(2)}) copy-start(bf16[512]{0:T(512)(128)(2,1)} %param.7) | copy-start | bytes 3076
  0.0 3.2 %copy-start = (s32[512]{0:T(512)S(1)}, s32[512]{0:T(512)}, u32[]{:S(2)}) copy-start(s32[512]{0:T(512)} %param.9) | copy-start | bytes 6148
  0.0 3.2 %copy-start.1 = (s32[512,1]{0,1:T(1,128)S(1)}, s32[512,1]{0,1:T(1,128)}, u32[]{:S(2)}) copy-start(s32[512,1]{0,1:T(1,128)} %param.8) | copy-start | bytes 6148
  2.6 1.7 %collective-permute-start = (f32[512,128]{1,0:T(8,128)S(1)}, f32[512,128]{1,0:T(8,128)S(1)}, u32[]{:S(2)}, u32[]{:S(2)}) collective-permute-start(f32[512,128]{1,0:T(8,128)S(1)} %get-tuple-element.21), channel_id=1, source_target_pairs={{0,1},{1,0},{2,3},{3,2},{4,5},{5,4},{6,7},{7,6},{8,9},{9,8},{10,11... | collective-permute-start | bytes 786440 | tf_op jit(solution)/shard_map/ppermute | solution.py:293

commit v3 on v2

--- a/solution.py
+++ b/solution.py
@@ -15,6 +15,9 @@
 VMEM = pl.BlockSpec(memory_space=pltpu.VMEM)
 HBM = pl.BlockSpec(memory_space=pltpu.HBM)
 CHUNKS = 1
+ROW_BLOCK = 512
+PICK_CHUNKS = 2
+SLAB = 2
 
 
 def grant(mebibytes):
@@ -37,7 +40,7 @@
     return jnp.sum(before * member, axis=0, keepdims=True).astype(jnp.int32)
 
 
-def project_kernel(stride, x_ref, loading_ref, cluster_ref, quality_ref, *refs):
+def project_kernel(cap, x_ref, loading_ref, cluster_ref, quality_ref, *refs):
     own_ref, weights_ref, place_ref, rank_ref, *out_refs, x_buf, labels, sems = refs
     parts = len(out_refs) + 1
     rows = own_ref.shape[0]
@@ -64,9 +67,9 @@
         copy.wait()
     cluster_row = labels[0]
     live = labels[1] == 1
-    rank = ranks(cluster_row, live, place_ref.shape[0] // stride)
+    rank = ranks(cluster_row, live, place_ref.shape[0] // cap)
     rank_ref[...] = jnp.broadcast_to(rank, rank_ref.shape)
-    place = jnp.where(live, cluster_row * stride + rank, -1)
+    place = jnp.where(live, cluster_row * cap + rank, -1)
     place_ref[...] = jnp.where(iota(place_ref.shape, 0) == place, 1.0, 0.0).astype(jnp.bfloat16)
     weights.wait()
     for p in range(parts):
@@ -78,18 +81,18 @@
             )
 
 
-def project(expression, loading, cluster, quality, parts, devices, stride):
+def project(expression, loading, cluster, quality, parts, devices, cap):
     cells, genes = expression.shape
     width = loading.shape[1]
     rows = cells // parts
     others = parts - 1
     operands = (expression, loading, cluster.reshape(1, rows), quality.reshape(1, rows))
     return pl.pallas_call(
-        functools.partial(project_kernel, stride),
+        functools.partial(project_kernel, cap),
         out_shape=[
             jax.ShapeDtypeStruct((rows, genes), expression.dtype),
             jax.ShapeDtypeStruct((genes, width), loading.dtype),
-            jax.ShapeDtypeStruct((devices * stride, rows), jnp.bfloat16),
+            jax.ShapeDtypeStruct((devices * cap, rows), jnp.bfloat16),
             jax.ShapeDtypeStruct((8, rows), jnp.int32),
         ]
         + [jax.ShapeDtypeStruct((rows, width), jnp.float32)] * others,
@@ -152,7 +155,7 @@
     )
 
 
-def pack_kernel(cap, place_ref, spare_ref, *refs):
+def pack_kernel(place_ref, spare_ref, *refs):
     *parts, packed_ref, embedded_ref = refs
     total = parts[0][...]
     for part in parts[1:]:
@@ -160,17 +163,19 @@
     embedded = total.astype(jnp.bfloat16)
     embedded_ref[...] = embedded
     rows = jnp.dot(place_ref[...], embedded, preferred_element_type=jnp.float32)
-    rows = rows.reshape(packed_ref.shape)
-    rows = jnp.where(iota(rows.shape, 1) >= cap, spare_ref[...][:, None, :], rows)
-    packed_ref[...] = rows.astype(jnp.bfloat16)
-
-
-def pack(parts, place, spare, cap, stride):
+    n_dest, slabs, slab, width = packed_ref.shape
+    rows = rows.reshape(n_dest, slabs - 1, slab, width)
+    packed_ref[:, : slabs - 1] = rows.astype(jnp.bfloat16)
+    spare = jnp.broadcast_to(spare_ref[...][:, None, None, :], (n_dest, 1, slab, width))
+    packed_ref[:, slabs - 1 :] = spare.astype(jnp.bfloat16)
+
+
+def pack(parts, place, spare, cap):
     cells, width = parts[0].shape
     return pl.pallas_call(
-        functools.partial(pack_kernel, cap),
+        pack_kernel,
         out_shape=[
-            jax.ShapeDtypeStruct((spare.shape[0], stride, width), jnp.bfloat16),
+            jax.ShapeDtypeStruct((spare.shape[0], cap // SLAB + 1, SLAB, width), jnp.bfloat16),
             jax.ShapeDtypeStruct((cells, width), jnp.bfloat16),
         ],
         in_specs=[VMEM] * (2 + len(parts)),
@@ -180,90 +185,97 @@
     )(place, spare, *parts)
 
 
-def diffuse_kernel(row_block, cap, arrived_ref, out_ref, left, right, gain, affinity, step):
-    sources = arrived_ref.shape[0]
-    slots = out_ref.shape[0]
+def diffuse_kernel(row_block, cap, arrived_ref, out_ref, rows, affinity, step):
+    slots, width = out_ref.shape
+    slabs = arrived_ref.shape[1] - 1
     groups = slots // LANES
     per = LANES // cap
-    widths = arrived_ref[:, cap, :].astype(jnp.float32).reshape(groups, per, LANES)
-    mine = lax.div(iota(widths.shape, 2), LANES // per) == iota(widths.shape, 1)
-    widths = jnp.sum(jnp.where(mine, widths, 0.0), axis=1)
-    present = widths > 0
-    inverse = jnp.where(present, 1.0 / jnp.where(present, widths, 1.0), 1.0)
-    absent_col = jnp.transpose(jnp.where(present, 0.0, 1.0))
-    gain_col = jnp.transpose(inverse * -LOG2E)
-    lane = iota((LANES, LANES), 1)
+    shape = (groups, LANES)
+    source = lax.div(iota(shape, 1), cap)
+    diagonal = iota((LANES, LANES), 0) == iota((LANES, LANES), 1)
+    widths = jnp.zeros(shape, jnp.float32)
+    half_norms = jnp.zeros(shape, jnp.float32)
+    rows[:, :width] = arrived_ref[:, :slabs].reshape(slots, width)
     for g in range(groups):
         block = pl.ds(g * LANES, LANES)
-        rows = jnp.concatenate(
-            [arrived_ref[s, :cap, :] for s in range(g * per, (g + 1) * per)], axis=0
+        line = jnp.zeros(shape, jnp.float32)
+        for q in range(per):
+            last = arrived_ref[g * per + q, slabs].astype(jnp.float32)[:1, :]
+            line = jnp.where(source == q, last, line)
+        embedded = rows[block, :width]
+        rows[block, width:] = jnp.ones((LANES, LANES), jnp.bfloat16)
+        own = lax.dot_general(embedded, embedded, NT, preferred_element_type=jnp.float32)
+        norm = jnp.sum(jnp.where(diagonal, own, 0.0), axis=0, keepdims=True)
+        here = iota(shape, 0) == g
+        widths = jnp.where(here, line, widths)
+        half_norms = jnp.where(here, 0.5 * norm, half_norms)
+    present = widths > 0
+    half_norms = jnp.where(present, half_norms, FAR)
+    inverse = jnp.where(present, 1.0 / jnp.where(present, widths, 1.0), 1.0)
+    norm_cols = jnp.transpose(half_norms)
+    gain_cols = jnp.transpose(inverse * (2.0 * LOG2E))
+
+    def across(lines):
+        return jnp.concatenate([lines[g : g + 1, :] for g in range(groups)], axis=1)
+
+    def down(cols, b):
+        first, count = b * row_block // LANES, row_block // LANES
+        return jnp.concatenate([cols[:, g : g + 1] for g in range(first, first + count)], axis=0)
+
+    norm_row, inverse_row = across(half_norms), across(inverse)
+    blocks = [pl.ds(b * row_block, row_block) for b in range(slots // row_block)]
+    one_steps, scales = [], []
+    for b, block in enumerate(blocks):
+        products = lax.dot_general(
+            rows[block, :width], rows[:, :width], NT, preferred_element_type=jnp.float32
         )
-        wide = rows.astype(jnp.float32)
-        norm = jnp.sum(wide * wide, axis=1, keepdims=True) + absent_col[:, g : g + 1] * FAR
-        high = norm.astype(jnp.bfloat16).astype(jnp.float32)
-        middle = (norm - high).astype(jnp.bfloat16).astype(jnp.float32)
-        low = norm - high - middle
-        one = jnp.ones_like(norm)
-        split = jnp.where(lane == 0, high, jnp.where(lane == 1, middle, low))
-        left[block, :LANES] = rows
-        right[block, :LANES] = (wide * -2.0).astype(jnp.bfloat16)
-        left[block, LANES:] = jnp.where(
-            lane < 3, split, jnp.where(lane < 6, one, 0.0)
-        ).astype(jnp.bfloat16)
-        split = jnp.where(lane == 3, high, jnp.where(lane == 4, middle, low))
-        right[block, LANES:] = jnp.where(
-            lane < 3, one, jnp.where(lane < 6, split, 0.0)
-        ).astype(jnp.bfloat16)
-        gain[block, :] = jnp.broadcast_to(gain_col[:, g : g + 1], (LANES, LANES))
-        step[block, :LANES] = rows
-        step[block, LANES:] = jnp.ones((LANES, LANES), jnp.bfloat16)
-    inverse_row = jnp.concatenate([inverse[g : g + 1, :] for g in range(groups)], axis=1)
-    blocks = [pl.ds(b * row_block, row_block) for b in range(slots // row_block)]
-    ones_steps, totals = [], []
-    for block in blocks:
-        distance = lax.dot_general(
-            left[block, :], right[...], NT, preferred_element_type=jnp.float32
-        )
-        power = distance * gain[block, :1] * inverse_row
+        power = (products - norm_row - down(norm_cols, b)) * (down(gain_cols, b) * inverse_row)
         weights = jnp.exp2(power).astype(jnp.bfloat16)
         affinity[block, :] = weights
-        both = jnp.dot(weights, step[...], preferred_element_type=jnp.float32)
-        total = both[:, LANES:]
-        total = jnp.where(total > 0, total, 1.0)
-        scale = 1.0 / total
-        ones_steps.append(0.5 * (left[block, :LANES].astype(jnp.float32) + both[:, :LANES] * scale))
-        totals.append(scale)
-    for block, one_step in zip(blocks, ones_steps):
-        step[block, :LANES] = one_step.astype(jnp.bfloat16)
-    for block, one_step, scale in zip(blocks, ones_steps, totals):
-        again = jnp.dot(affinity[block, :], step[:, :LANES], preferred_element_type=jnp.float32)
+        both = jnp.dot(weights, rows[...], preferred_element_type=jnp.float32)
+        total = both[:, width:]
+        scale = 1.0 / jnp.where(total > 0, total, 1.0)
+        one_step = 0.5 * (rows[block, :width].astype(jnp.float32) + both[:, :width] * scale)
+        step[block, :] = one_step.astype(jnp.bfloat16)
+        one_steps.append(one_step)
+        scales.append(scale)
+    for block, one_step, scale in zip(blocks, one_steps, scales):
+        again = jnp.dot(affinity[block, :], step[...], preferred_element_type=jnp.float32)
         out_ref[block, :] = (0.5 * (one_step + again * scale)).astype(out_ref.dtype)
 
 
 def diffuse(arrived, cap):
-    sources, _, width = arrived.shape
+    sources, _, _, width = arrived.shape
     slots = sources * cap
     return pl.pallas_call(
-        functools.partial(diffuse_kernel, 256, cap),
+        functools.partial(diffuse_kernel, ROW_BLOCK, cap),
         out_shape=jax.ShapeDtypeStruct((slots, width), jnp.bfloat16),
         in_specs=[VMEM],
         out_specs=VMEM,
         scratch_shapes=[
-            pltpu.VMEM((slots, 2 * width), jnp.bfloat16),
-            pltpu.VMEM((slots, 2 * width), jnp.bfloat16),
-            pltpu.VMEM((slots, LANES), jnp.float32),
+            pltpu.VMEM((slots, width + LANES), jnp.bfloat16),
             pltpu.VMEM((slots, slots), jnp.bfloat16),
-            pltpu.VMEM((slots, 2 * width), jnp.bfloat16),
+            pltpu.VMEM((slots, width), jnp.bfloat16),
         ],
         compiler_params=grant(16),
         name="diffuse",
     )(arrived)
 
 
-def pick_kernel(quality_ref, pick_ref, returned_ref, embedded_ref, out_ref):
-    picked = jnp.dot(pick_ref[...], returned_ref[...], preferred_element_type=jnp.float32)
-    live = jnp.transpose(jnp.broadcast_to(quality_ref[...], (8, out_ref.shape[0])))[:, :1] == 1
-    out_ref[...] = jnp.where(live, picked, embedded_ref[...].astype(jnp.float32))
+def pick_kernel(quality_ref, pick_ref, returned_ref, embedded_ref, out_ref, buf, sems):
+    cells = out_ref.shape[0]
+    live = jnp.transpose(jnp.broadcast_to(quality_ref[...], (8, cells)))[:, :1] == 1
+    depth = cells // PICK_CHUNKS
+    copies = []
+    for k in range(PICK_CHUNKS):
+        block = pl.ds(k * depth, depth)
+        picked = jnp.dot(pick_ref[block, :], returned_ref[...], preferred_element_type=jnp.float32)
+        kept = embedded_ref[block, :].astype(jnp.float32)
+        buf[block, :] = jnp.where(live[k * depth : (k + 1) * depth], picked, kept)
+        copies.append(pltpu.make_async_copy(buf.at[block, :], out_ref.at[block, :], sems.at[k]))
+        copies[k].start()
+    for copy in copies:
+        copy.wait()
 
 
 def pick(quality, pick_onehot, returned, embedded):
@@ -272,7 +284,11 @@
         pick_kernel,
         out_shape=jax.ShapeDtypeStruct((cells, width), jnp.float32),
         in_specs=[VMEM] * 4,
-        out_specs=VMEM,
+        out_specs=HBM,
+        scratch_shapes=[
+            pltpu.VMEM((cells, width), jnp.float32),
+            pltpu.SemaphoreType.DMA((PICK_CHUNKS,)),
+        ],
         compiler_params=grant(8),
         name="pick",
     )(quality.reshape(1, cells), pick_onehot, returned, embedded)
@@ -281,11 +297,10 @@
 def body(expression, loading, kernel_width, cluster, quality):
     gene_count = lax.axis_size("genes")
     devices = gene_count * lax.axis_size("cells")
-    cap = max(1, 2 * kernel_width.shape[0] // devices)
-    stride = 8 * (cap // 8 + 1)
+    cap = SLAB * pl.cdiv(max(1, 2 * kernel_width.shape[0] // devices), SLAB)
     width = loading.shape[1]
     own, weights, place, rank, *partials = project(
-        expression, loading, cluster, quality, gene_count, devices, stride
+        expression, loading, cluster, quality, gene_count, devices, cap
     )
     parts = []
     for shift, partial in enumerate(partials, 1):
@@ -295,7 +310,7 @@
         own, weights, cluster, quality, rank, kernel_width, devices, cap
     )
     parts.append(own_part)
-    packed, embedded = pack(parts, place, spare, cap, stride)
+    packed, embedded = pack(parts, place, spare, cap)
     arrived = lax.all_to_all(packed, AXES, split_axis=0, concat_axis=0, tiled=True)
     smoothed = diffuse(arrived, cap)
     returned = lax.all_to_all(

time: 41 us -> 39.3 us (0.959)
  blocking collectives: 31.8 us -> 30.7 us
  Pallas kernels: 8.12 us -> 7.53 us
    all_to_all x1, blocking collectives: 19.1 us -> 18.1 us  [body(): lax.all_to_all(packed, AXES, split_axis=0, concat_axis=0, tiled=True)]
    pallas_call x3, Pallas kernels: 6.06 us -> 5.54 us  [the longest x1 2.59 us: project(): pl.pallas_call(functools.partial(project_kernel, cap), out_shape=[jax.Sha...]
where the time goes in v3:
time: 39.3 us; the launch traced here: 39.2 us
  blocking collectives  30.7 us (78%)
  Pallas kernels  7.53 us (19%)
  starting transfers between devices  0.57 us (1%)
    all_to_all x1, blocking collectives, body(): lax.all_to_all(packed, AXES, split_axis=0, concat_axis=0, tiled=True)  18.1 us
    all_to_all x1, blocking collectives, body(): lax.all_to_all(smoothed.reshape(devices, cap, width), AXES, split_axis=0,...  12.6 us
    pallas_call x1, Pallas kernels, project(): pl.pallas_call(functools.partial(project_kernel, cap), out_shape=[jax.Sha...  2.59 us
    pallas_call x1, Pallas kernels, diffuse(): pl.pallas_call(functools.partial(diffuse_kernel, ROW_BLOCK, cap), out_sha...  2.5 us
    pallas_call x1, Pallas kernels, pick(): pl.pallas_call(pick_kernel, out_shape=jax.ShapeDtypeStruct((cells, width)...  1.15 us
    pallas_call x1, Pallas kernels, project_own(): pl.pallas_call(functools.partial(project_own_kernel, cap), out_shape=[jax...  0.84 us
  transfers between devices with their start and end apart: 1, of which 1 were waited for; matrix products, arithmetic and copies ran while one was open for 0% of the time, Pallas kernels for 2%

profile of v3, /device:TPU:0, one launch (start us, length us, event | category | flops | bytes accessed | tf_op | source)
XLA Modules:
  0.0 39.2 jit_solution(3661659993067406132)
XLA Ops:
  0.0 0.0 copy-start
  0.0 0.0 copy-start.1
  0.0 0.0 copy-start.2
  0.0 2.6 %project.1 = (bf16[512,2048]{1,0:T(8,128)(2,1)S(1)}, bf16[2048,128]{1,0:T(8,128)(2,1)S(1)}, bf16[1024,512]{1,0:T(8,128)(2,1)S(1)}, s32[8,512]{1,0:T(8,128)S(1)}, f32[512,128]{1,0:T(8,128)S(1)}) custom-call(bf16[1024,2048]{1,0:T(8,128)(2,1)} %x_ref.1, bf16[2048,128]{1,0:T(8,128)(2,1)} %loading_ref.1, s32[1,512]{1,0:T(1,128)} %bitcast.9, s32[1,512]{1,0:T(1,128)} %bitcast.6), custom_call_target="tpu_custom_call" | custom-call | tf_op jit(solution)/shard_map/project/pallas_call | solution.py:90
  2.6 0.6 %collective-permute-start = (f32[512,128]{1,0:T(8,128)S(1)}, f32[512,128]{1,0:T(8,128)S(1)}, u32[]{:S(2)}, u32[]{:S(2)}) collective-permute-start(f32[512,128]{1,0:T(8,128)S(1)} %get-tuple-element.21), channel_id=1, source_target_pairs={{0,1},{1,0},{2,3},{3,2},{4,5},{5,4},{6,7},{7,6},{8,9},{9,8},{10,11... | collective-permute-start | bytes 786440 | tf_op jit(solution)/shard_map/ppermute | solution.py:308
  3.2 0.0 copy-done.2
  3.2 0.0 copy-done
  3.2 0.0 copy-done.1
  3.2 0.8 %project_own.1 = (f32[512,128]{1,0:T(8,128)S(1)}, f32[32,128]{1,0:T(8,128)S(1)}, bf16[512,1024]{1,0:T(8,128)(2,1)S(1)}) custom-call(bf16[512,2048]{1,0:T(8,128)(2,1)S(1)} %get-tuple-element.15.x_ref, bf16[2048,128]{1,0:T(8,128)(2,1)S(1)} %get-tuple-element.16.weights_ref, s32[1,512]{1,0:T(1,128)S(1)} %bitcast.10, s32[1,512]{1,0:T(1,128)S(1)} %bitcast.7, ...), custom_call_target="tpu_custom_call" | custom-call | flops 268435456 | bytes 2621440 | tf_op jit(solution)/shard_map/project_own/pallas_call | solution.py:132
  4.0 0.3 collective-permute-done.refs_0_
  4.3 0.4 %pack.1 = (bf16[32,17,2,128]{3,2,1,0:T(2,128)(2,1)S(1)}, bf16[512,128]{1,0:T(8,128)(2,1)S(1)}) custom-call(bf16[1024,512]{1,0:T(8,128)(2,1)S(1)} %get-tuple-element.19.place_ref, f32[32,128]{1,0:T(8,128)S(1)} %get-tuple-element.20.spare_ref, f32[512,128]{1,0:T(8,128)S(1)} %collective-permute-done.refs_0_, f32[512,128]{1,0:T(8,128)S(1)} %get-tuple-element.22.refs_1_), custom_call_target="tpu_custom_call" | custom-call | tf_op jit(solution)/shard_map/pack/pallas_call | solution.py:175
  4.8 18.1 %all_to_all.10.arrived_ref = bf16[32,17,2,128]{3,2,1,0:T(2,128)(2,1)S(1)} all-to-all(bf16[32,17,2,128]{3,2,1,0:T(2,128)(2,1)S(1)} %get-tuple-element.23), channel_id=1, replica_groups=mesh['cells'=16,'genes'=2] {'cells','genes'}, dimensions={0} | all-to-all | bytes 557056 | tf_op jit(solution)/shard_map/all_to_all | solution.py:314
  22.9 2.5 %diffuse.1 = bf16[1024,128]{1,0:T(8,128)(2,1)S(1)} custom-call(bf16[32,17,2,128]{3,2,1,0:T(2,128)(2,1)S(1)} %all_to_all.10.arrived_ref), custom_call_target="tpu_custom_call" | custom-call | tf_op jit(solution)/shard_map/diffuse/pallas_call | solution.py:250
  25.4 12.6 %all_to_all.11 = bf16[32,32,128]{2,1,0:T(8,128)(2,1)S(1)} all-to-all(bf16[32,32,128]{2,1,0:T(8,128)(2,1)S(1)} %bitcast.4), channel_id=1, replica_groups=mesh['cells'=16,'genes'=2] {'cells','genes'}, dimensions={0} | all-to-all | bytes 524288 | tf_op jit(solution)/shard_map/all_to_all | solution.py:316
  38.0 1.1 %pick.1 = f32[512,128]{1,0:T(8,128)} custom-call(s32[1,512]{1,0:T(1,128)S(1)} %bitcast.8, bf16[512,1024]{1,0:T(8,128)(2,1)S(1)} %get-tuple-element.18.pick_ref, bf16[1024,128]{1,0:T(8,128)(2,1)S(1)} %bitcast.5, bf16[512,128]{1,0:T(8,128)(2,1)S(1)} %get-tuple-element.24.embedded_ref), custom_call_target="tpu_custom_call" | custom-call | tf_op jit(solution)/shard_map/pick/pallas_call | solution.py:283
  (1 shorter events, 0.0 us)
Async XLA Ops:
  0.0 3.2 %copy-start = (s32[512]{0:T(512)S(1)}, s32[512]{0:T(512)}, u32[]{:S(2)}) copy-start(s32[512]{0:T(512)} %param.9) | copy-start | bytes 6148
  0.0 3.2 %copy-start.1 = (s32[512,1]{0,1:T(1,128)S(1)}, s32[512,1]{0,1:T(1,128)}, u32[]{:S(2)}) copy-start(s32[512,1]{0,1:T(1,128)} %param.8) | copy-start | bytes 6148
  0.0 3.2 %copy-start.2 = (bf16[512]{0:T(512)(128)(2,1)S(1)}, bf16[512]{0:T(512)(128)(2,1)}, u32[]{:S(2)}) copy-start(bf16[512]{0:T(512)(128)(2,1)} %param.7) | copy-start | bytes 3076
  2.6 1.7 %collective-permute-start = (f32[512,128]{1,0:T(8,128)S(1)}, f32[512,128]{1,0:T(8,128)S(1)}, u32[]{:S(2)}, u32[]{:S(2)}) collective-permute-start(f32[512,128]{1,0:T(8,128)S(1)} %get-tuple-element.21), channel_id=1, source_target_pairs={{0,1},{1,0},{2,3},{3,2},{4,5},{5,4},{6,7},{7,6},{8,9},{9,8},{10,11... | collective-permute-start | bytes 786440 | tf_op jit(solution)/shard_map/ppermute | solution.py:308

commit v4 on v3

--- a/solution.py
+++ b/solution.py
@@ -15,7 +15,8 @@
 VMEM = pl.BlockSpec(memory_space=pltpu.VMEM)
 HBM = pl.BlockSpec(memory_space=pltpu.HBM)
 CHUNKS = 1
-ROW_BLOCK = 512
+ROW_BLOCK = 256
+TALL_BLOCKS = 2
 PICK_CHUNKS = 2
 SLAB = 2
 
@@ -67,9 +68,10 @@
         copy.wait()
     cluster_row = labels[0]
     live = labels[1] == 1
-    rank = ranks(cluster_row, live, place_ref.shape[0] // cap)
+    half = place_ref.shape[0]
+    rank = ranks(cluster_row, live, 2 * half // cap)
     rank_ref[...] = jnp.broadcast_to(rank, rank_ref.shape)
-    place = jnp.where(live, cluster_row * cap + rank, -1)
+    place = jnp.where(live, lax.rem(cluster_row * cap + rank, half), -1)
     place_ref[...] = jnp.where(iota(place_ref.shape, 0) == place, 1.0, 0.0).astype(jnp.bfloat16)
     weights.wait()
     for p in range(parts):
@@ -92,7 +94,7 @@
         out_shape=[
             jax.ShapeDtypeStruct((rows, genes), expression.dtype),
             jax.ShapeDtypeStruct((genes, width), loading.dtype),
-            jax.ShapeDtypeStruct((devices * cap, rows), jnp.bfloat16),
+            jax.ShapeDtypeStruct((devices * cap // 2, rows), jnp.bfloat16),
             jax.ShapeDtypeStruct((8, rows), jnp.int32),
         ]
         + [jax.ShapeDtypeStruct((rows, width), jnp.float32)] * others,
@@ -109,7 +111,7 @@
 
 
 def project_own_kernel(cap, x_ref, weights_ref, cluster_ref, quality_ref, rank_ref, width_ref, *refs):
-    out_ref, spare_ref, pick_ref = refs
+    out_ref, spare_ref, pick_ref, side_ref = refs
     out_ref[...] = jnp.dot(x_ref[...], weights_ref[...], preferred_element_type=jnp.float32)
     cells = x_ref.shape[0]
     live = quality_ref[...] == 1
@@ -117,7 +119,11 @@
     rank = rank_ref[:1, :]
     slot = jnp.where(live, cluster_ref[...] * cap + rank, -1)
     slot = jnp.transpose(jnp.broadcast_to(slot, (8, cells)))[:, :1]
-    pick_ref[...] = jnp.where(iota(pick_ref.shape, 1) == slot, 1.0, 0.0).astype(jnp.bfloat16)
+    half = pick_ref.shape[1]
+    side = jnp.where(slot < 0, -1, jnp.where(slot < half, 0, 1))
+    side_ref[...] = jnp.broadcast_to(side, side_ref.shape)
+    place = slot - jnp.maximum(side, 0) * half
+    pick_ref[...] = jnp.where(iota(pick_ref.shape, 1) == place, 1.0, 0.0).astype(jnp.bfloat16)
     member = iota((spare_ref.shape[0], cells), 0) == cluster_ref[...]
     owned = jnp.where(member, widths, 0.0).astype(jnp.bfloat16)
     same_rank = jnp.where(lax.rem(iota((LANES, cells), 0), cap) == rank, 1.0, 0.0)
@@ -134,10 +140,11 @@
         out_shape=[
             jax.ShapeDtypeStruct((rows, width), jnp.float32),
             jax.ShapeDtypeStruct((devices, LANES), jnp.float32),
-            jax.ShapeDtypeStruct((rows, devices * cap), jnp.bfloat16),
+            jax.ShapeDtypeStruct((rows, devices * cap // 2), jnp.bfloat16),
+            jax.ShapeDtypeStruct((rows, width), jnp.int32),
         ],
         in_specs=[VMEM] * 6,
-        out_specs=[VMEM] * 3,
+        out_specs=[VMEM] * 4,
         cost_estimate=pl.CostEstimate(
             flops=2 * rows * genes * width,
             bytes_accessed=2 * genes * (rows + width),
@@ -155,22 +162,27 @@
     )
 
 
-def pack_kernel(place_ref, spare_ref, *refs):
+def pack_kernel(place_ref, side_ref, spare_ref, *refs):
     *parts, packed_ref, embedded_ref = refs
     total = parts[0][...]
     for part in parts[1:]:
         total = total + part[...]
     embedded = total.astype(jnp.bfloat16)
     embedded_ref[...] = embedded
-    rows = jnp.dot(place_ref[...], embedded, preferred_element_type=jnp.float32)
+    side = side_ref[...]
+    halves = [jnp.where(side == half, total, 0.0).astype(jnp.bfloat16) for half in range(2)]
+    both = jnp.concatenate(halves, axis=1)
+    rows = jnp.dot(place_ref[...], both, preferred_element_type=jnp.float32)
     n_dest, slabs, slab, width = packed_ref.shape
-    rows = rows.reshape(n_dest, slabs - 1, slab, width)
-    packed_ref[:, : slabs - 1] = rows.astype(jnp.bfloat16)
+    for half in range(2):
+        part = rows[:, half * width : (half + 1) * width].astype(jnp.bfloat16)
+        part = part.reshape(n_dest // 2, slabs - 1, slab, width)
+        packed_ref[half * n_dest // 2 : (half + 1) * n_dest // 2, : slabs - 1] = part
     spare = jnp.broadcast_to(spare_ref[...][:, None, None, :], (n_dest, 1, slab, width))
     packed_ref[:, slabs - 1 :] = spare.astype(jnp.bfloat16)
 
 
-def pack(parts, place, spare, cap):
+def pack(parts, place, side, spare, cap):
     cells, width = parts[0].shape
     return pl.pallas_call(
         pack_kernel,
@@ -178,11 +190,11 @@
             jax.ShapeDtypeStruct((spare.shape[0], cap // SLAB + 1, SLAB, width), jnp.bfloat16),
             jax.ShapeDtypeStruct((cells, width), jnp.bfloat16),
         ],
-        in_specs=[VMEM] * (2 + len(parts)),
+        in_specs=[VMEM] * (3 + len(parts)),
         out_specs=[VMEM] * 2,
         compiler_params=grant(10),
         name="pack",
-    )(place, spare, *parts)
+    )(place, side, spare, *parts)
 
 
 def diffuse_kernel(row_block, cap, arrived_ref, out_ref, rows, affinity, step):
@@ -226,12 +238,20 @@
     blocks = [pl.ds(b * row_block, row_block) for b in range(slots // row_block)]
     one_steps, scales = [], []
     for b, block in enumerate(blocks):
+        first = b * row_block
+        beyond = pl.ds(first, slots - first)
         products = lax.dot_general(
-            rows[block, :width], rows[:, :width], NT, preferred_element_type=jnp.float32
+            rows[block, :width], rows[beyond, :width], NT, preferred_element_type=jnp.float32
         )
-        power = (products - norm_row - down(norm_cols, b)) * (down(gain_cols, b) * inverse_row)
+        power = (products - norm_row[:, first:] - down(norm_cols, b)) * (
+            down(gain_cols, b) * inverse_row[:, first:]
+        )
         weights = jnp.exp2(power).astype(jnp.bfloat16)
-        affinity[block, :] = weights
+        affinity[block, beyond] = weights
+        for later in range(b + 1, len(blocks)):
+            start = (later - b) * row_block
+            affinity[blocks[later], block] = jnp.transpose(weights[:, start : start + row_block])
+        weights = affinity[block, :]
         both = jnp.dot(weights, rows[...], preferred_element_type=jnp.float32)
         total = both[:, width:]
         scale = 1.0 / jnp.where(total > 0, total, 1.0)
@@ -239,9 +259,15 @@
         step[block, :] = one_step.astype(jnp.bfloat16)
         one_steps.append(one_step)
         scales.append(scale)
-    for block, one_step, scale in zip(blocks, one_steps, scales):
+    tall = slots // TALL_BLOCKS
+    join = len(blocks) // TALL_BLOCKS
+    for t in range(TALL_BLOCKS):
+        block = pl.ds(t * tall, tall)
         again = jnp.dot(affinity[block, :], step[...], preferred_element_type=jnp.float32)
-        out_ref[block, :] = (0.5 * (one_step + again * scale)).astype(out_ref.dtype)
+        for b in range(t * join, (t + 1) * join):
+            start = b * row_block - t * tall
+            more = again[start : start + row_block] * scales[b]
+            out_ref[blocks[b], :] = (0.5 * (one_steps[b] + more)).astype(out_ref.dtype)
 
 
 def diffuse(arrived, cap):
@@ -262,23 +288,26 @@
     )(arrived)
 
 
-def pick_kernel(quality_ref, pick_ref, returned_ref, embedded_ref, out_ref, buf, sems):
-    cells = out_ref.shape[0]
-    live = jnp.transpose(jnp.broadcast_to(quality_ref[...], (8, cells)))[:, :1] == 1
+def pick_kernel(pick_ref, side_ref, returned_ref, embedded_ref, out_ref, buf, sems):
+    cells, width = out_ref.shape
+    half = pick_ref.shape[1]
+    both = jnp.concatenate([returned_ref[:half, :], returned_ref[half:, :]], axis=1)
     depth = cells // PICK_CHUNKS
     copies = []
     for k in range(PICK_CHUNKS):
         block = pl.ds(k * depth, depth)
-        picked = jnp.dot(pick_ref[block, :], returned_ref[...], preferred_element_type=jnp.float32)
+        picked = jnp.dot(pick_ref[block, :], both, preferred_element_type=jnp.float32)
+        side = side_ref[block, :]
         kept = embedded_ref[block, :].astype(jnp.float32)
-        buf[block, :] = jnp.where(live[k * depth : (k + 1) * depth], picked, kept)
+        second = jnp.where(side == 1, picked[:, width:], kept)
+        buf[block, :] = jnp.where(side == 0, picked[:, :width], second)
         copies.append(pltpu.make_async_copy(buf.at[block, :], out_ref.at[block, :], sems.at[k]))
         copies[k].start()
     for copy in copies:
         copy.wait()
 
 
-def pick(quality, pick_onehot, returned, embedded):
+def pick(pick_onehot, side, returned, embedded):
     cells, width = embedded.shape
     return pl.pallas_call(
         pick_kernel,
@@ -291,7 +320,7 @@
         ],
         compiler_params=grant(8),
         name="pick",
-    )(quality.reshape(1, cells), pick_onehot, returned, embedded)
+    )(pick_onehot, side, returned, embedded)
 
 
 def body(expression, loading, kernel_width, cluster, quality):
@@ -306,17 +335,17 @@
     for shift, partial in enumerate(partials, 1):
         ring = [(i, (i + shift) % gene_count) for i in range(gene_count)]
         parts.append(lax.ppermute(partial, "genes", ring))
-    own_part, spare, pick_onehot = project_own(
+    own_part, spare, pick_onehot, side = project_own(
         own, weights, cluster, quality, rank, kernel_width, devices, cap
     )
     parts.append(own_part)
-    packed, embedded = pack(parts, place, spare, cap)
+    packed, embedded = pack(parts, place, side, spare, cap)
     arrived = lax.all_to_all(packed, AXES, split_axis=0, concat_axis=0, tiled=True)
     smoothed = diffuse(arrived, cap)
     returned = lax.all_to_all(
         smoothed.reshape(devices, cap, width), AXES, split_axis=0, concat_axis=0, tiled=True
     )
-    return pick(quality, pick_onehot, returned.reshape(devices * cap, width), embedded)
+    return pick(pick_onehot, side, returned.reshape(devices * cap, width), embedded)
 
 
 def solution(mesh):

time: 39.3 us -> 38.7 us (0.985)
  Pallas kernels: 7.53 us -> 6.89 us
where the time goes in v4:
time: 38.7 us; the launch traced here: 38.6 us
  blocking collectives  30.7 us (79%)
  Pallas kernels  6.89 us (18%)
  starting transfers between devices  0.57 us (1%)
    all_to_all x1, blocking collectives, body(): lax.all_to_all(packed, AXES, split_axis=0, concat_axis=0, tiled=True)  18.1 us
    all_to_all x1, blocking collectives, body(): lax.all_to_all(smoothed.reshape(devices, cap, width), AXES, split_axis=0,...  12.6 us
    pallas_call x1, Pallas kernels, project(): pl.pallas_call(functools.partial(project_kernel, cap), out_shape=[jax.Sha...  2.59 us
    pallas_call x1, Pallas kernels, diffuse(): pl.pallas_call(functools.partial(diffuse_kernel, ROW_BLOCK, cap), out_sha...  2.11 us
    pallas_call x1, Pallas kernels, pick(): pl.pallas_call(pick_kernel, out_shape=jax.ShapeDtypeStruct((cells, width)...  1.02 us
    pallas_call x1, Pallas kernels, project_own(): pl.pallas_call(functools.partial(project_own_kernel, cap), out_shape=[jax...  0.81 us
  transfers between devices with their start and end apart: 1, of which 1 were waited for; matrix products, arithmetic and copies ran while one was open for 0% of the time, Pallas kernels for 2%

profile of v4, /device:TPU:0, one launch (start us, length us, event | category | flops | bytes accessed | tf_op | source)
XLA Modules:
  0.0 38.6 jit_solution(16663538410323884451)
XLA Ops:
  0.0 0.0 copy-start.1
  0.0 0.0 copy-start
  0.0 0.0 copy-start.2
  0.0 2.6 %project.1 = (bf16[512,2048]{1,0:T(8,128)(2,1)S(1)}, bf16[2048,128]{1,0:T(8,128)(2,1)S(1)}, bf16[512,512]{1,0:T(8,128)(2,1)S(1)}, s32[8,512]{1,0:T(8,128)S(1)}, f32[512,128]{1,0:T(8,128)S(1)}) custom-call(bf16[1024,2048]{1,0:T(8,128)(2,1)} %x_ref.1, bf16[2048,128]{1,0:T(8,128)(2,1)} %loading_ref.1, s32[1,512]{1,0:T(1,128)} %bitcast.6, s32[1,512]{1,0:T(1,128)} %bitcast.8), custom_call_target="tpu_custom_call" | custom-call | tf_op jit(solution)/shard_map/project/pallas_call | solution.py:92
  2.6 0.6 %collective-permute-start = (f32[512,128]{1,0:T(8,128)S(1)}, f32[512,128]{1,0:T(8,128)S(1)}, u32[]{:S(2)}, u32[]{:S(2)}) collective-permute-start(f32[512,128]{1,0:T(8,128)S(1)} %get-tuple-element.23), channel_id=1, source_target_pairs={{0,1},{1,0},{2,3},{3,2},{4,5},{5,4},{6,7},{7,6},{8,9},{9,8},{10,11... | collective-permute-start | bytes 786440 | tf_op jit(solution)/shard_map/ppermute | solution.py:337
  3.2 0.0 copy-done.2
  3.2 0.0 copy-done.1
  3.2 0.0 copy-done
  3.2 0.8 %project_own.1 = (f32[512,128]{1,0:T(8,128)S(1)}, f32[32,128]{1,0:T(8,128)S(1)}, bf16[512,512]{1,0:T(8,128)(2,1)S(1)}, s32[512,128]{1,0:T(8,128)S(1)}) custom-call(bf16[512,2048]{1,0:T(8,128)(2,1)S(1)} %get-tuple-element.16.x_ref, bf16[2048,128]{1,0:T(8,128)(2,1)S(1)} %get-tuple-element.17.weights_ref, s32[1,512]{1,0:T(1,128)S(1)} %bitcast.7, ...), custom_call_target="tpu_custom_call" | custom-call | flops 268435456 | bytes 2621440 | tf_op jit(solution)/shard_map/project_own/pallas_call | solution.py:138
  4.0 0.3 collective-permute-done.refs_0_
  4.3 0.4 pack.1
  4.7 18.1 %all_to_all.10.arrived_ref = bf16[32,17,2,128]{3,2,1,0:T(2,128)(2,1)S(1)} all-to-all(bf16[32,17,2,128]{3,2,1,0:T(2,128)(2,1)S(1)} %get-tuple-element.25), channel_id=1, replica_groups=mesh['cells'=16,'genes'=2] {'cells','genes'}, dimensions={0} | all-to-all | bytes 557056 | tf_op jit(solution)/shard_map/all_to_all | solution.py:343
  22.8 2.1 %diffuse.1 = bf16[1024,128]{1,0:T(8,128)(2,1)S(1)} custom-call(bf16[32,17,2,128]{3,2,1,0:T(2,128)(2,1)S(1)} %all_to_all.10.arrived_ref), custom_call_target="tpu_custom_call" | custom-call | tf_op jit(solution)/shard_map/diffuse/pallas_call | solution.py:276
  24.9 12.6 %all_to_all.11 = bf16[32,32,128]{2,1,0:T(8,128)(2,1)S(1)} all-to-all(bf16[32,32,128]{2,1,0:T(8,128)(2,1)S(1)} %bitcast.4), channel_id=1, replica_groups=mesh['cells'=16,'genes'=2] {'cells','genes'}, dimensions={0} | all-to-all | bytes 524288 | tf_op jit(solution)/shard_map/all_to_all | solution.py:345
  37.5 1.0 %pick.1 = f32[512,128]{1,0:T(8,128)} custom-call(bf16[512,512]{1,0:T(8,128)(2,1)S(1)} %get-tuple-element.19.pick_ref, s32[512,128]{1,0:T(8,128)S(1)} %get-tuple-element.20.side_ref, bf16[1024,128]{1,0:T(8,128)(2,1)S(1)} %bitcast.5, bf16[512,128]{1,0:T(8,128)(2,1)S(1)} %get-tuple-element.26.embedded_ref), custom_call_target="tpu_custom_call" | custom-call | tf_op jit(solution)/shard_map/pick/pallas_call | solution.py:312
  (1 shorter events, 0.0 us)
Async XLA Ops:
  0.0 3.2 %copy-start.1 = (s32[512]{0:T(512)S(1)}, s32[512]{0:T(512)}, u32[]{:S(2)}) copy-start(s32[512]{0:T(512)} %param.9) | copy-start | bytes 6148
  0.0 3.2 %copy-start = (s32[512,1]{0,1:T(1,128)S(1)}, s32[512,1]{0,1:T(1,128)}, u32[]{:S(2)}) copy-start(s32[512,1]{0,1:T(1,128)} %param.8) | copy-start | bytes 6148
  0.0 3.2 %copy-start.2 = (bf16[512]{0:T(512)(128)(2,1)S(1)}, bf16[512]{0:T(512)(128)(2,1)}, u32[]{:S(2)}) copy-start(bf16[512]{0:T(512)(128)(2,1)} %param.7) | copy-start | bytes 3076
  2.6 1.7 %collective-permute-start = (f32[512,128]{1,0:T(8,128)S(1)}, f32[512,128]{1,0:T(8,128)S(1)}, u32[]{:S(2)}, u32[]{:S(2)}) collective-permute-start(f32[512,128]{1,0:T(8,128)S(1)} %get-tuple-element.23), channel_id=1, source_target_pairs={{0,1},{1,0},{2,3},{3,2},{4,5},{5,4},{6,7},{7,6},{8,9},{9,8},{10,11... | collective-permute-start | bytes 786440 | tf_op jit(solution)/shard_map/ppermute | solution.py:337

commit v5 on v4

--- a/solution.py
+++ b/solution.py
@@ -14,7 +14,7 @@
 NT = (((1,), (1,)), ((), ()))
 VMEM = pl.BlockSpec(memory_space=pltpu.VMEM)
 HBM = pl.BlockSpec(memory_space=pltpu.HBM)
-CHUNKS = 1
+CHUNKS = 2
 ROW_BLOCK = 256
 TALL_BLOCKS = 2
 PICK_CHUNKS = 2
@@ -56,7 +56,7 @@
         copy.start()
     copies = []
     for p in range(parts):
-        buffer = own_ref if p == parts - 1 else x_buf.at[p]
+        buffer = own_ref if p == parts - 1 else x_buf.at[pl.ds(p * rows, rows), :]
         first = lax.rem(me + p + 1, parts) * rows
         copies.append([])
         for c in range(CHUNKS):
@@ -75,12 +75,14 @@
     place_ref[...] = jnp.where(iota(place_ref.shape, 0) == place, 1.0, 0.0).astype(jnp.bfloat16)
     weights.wait()
     for p in range(parts):
-        for copy in copies[p]:
+        for c, copy in enumerate(copies[p]):
             copy.wait()
-        if p < parts - 1:
-            out_refs[p][...] = jnp.dot(
-                x_buf[p], weights_ref[...], preferred_element_type=jnp.float32
-            )
+            if p < parts - 1:
+                out_refs[p][pl.ds(c * depth, depth), :] = jnp.dot(
+                    x_buf[pl.ds(p * rows + c * depth, depth), :],
+                    weights_ref[...],
+                    preferred_element_type=jnp.float32,
+                )
 
 
 def project(expression, loading, cluster, quality, parts, devices, cap):
@@ -101,7 +103,7 @@
         in_specs=[HBM] * 4,
         out_specs=[VMEM] * (4 + others),
         scratch_shapes=[
-            pltpu.VMEM((max(others, 1), rows, genes), expression.dtype),
+            pltpu.VMEM((max(others, 1) * rows, genes), expression.dtype),
             pltpu.VMEM((2, 1, rows), jnp.int32),
             pltpu.SemaphoreType.DMA((parts + 1, CHUNKS + 1)),
         ],
@@ -204,7 +206,6 @@
     per = LANES // cap
     shape = (groups, LANES)
     source = lax.div(iota(shape, 1), cap)
-    diagonal = iota((LANES, LANES), 0) == iota((LANES, LANES), 1)
     widths = jnp.zeros(shape, jnp.float32)
     half_norms = jnp.zeros(shape, jnp.float32)
     rows[:, :width] = arrived_ref[:, :slabs].reshape(slots, width)
@@ -216,8 +217,8 @@
             line = jnp.where(source == q, last, line)
         embedded = rows[block, :width]
         rows[block, width:] = jnp.ones((LANES, LANES), jnp.bfloat16)
-        own = lax.dot_general(embedded, embedded, NT, preferred_element_type=jnp.float32)
-        norm = jnp.sum(jnp.where(diagonal, own, 0.0), axis=0, keepdims=True)
+        wide = embedded.astype(jnp.float32)
+        norm = jnp.sum(jnp.transpose(wide * wide), axis=0, keepdims=True)
         here = iota(shape, 0) == g
         widths = jnp.where(here, line, widths)
         half_norms = jnp.where(here, 0.5 * norm, half_norms)

time: 38.7 us -> 38.6 us (level)
  no operation moved by 1% of the time
where the time goes in v5:
time: 38.6 us; the launch traced here: 38.4 us
  blocking collectives  30.7 us (80%)
  Pallas kernels  6.75 us (17%)
  starting transfers between devices  0.56 us (1%)
    all_to_all x1, blocking collectives, body(): lax.all_to_all(packed, AXES, split_axis=0, concat_axis=0, tiled=True)  18.1 us
    all_to_all x1, blocking collectives, body(): lax.all_to_all(smoothed.reshape(devices, cap, width), AXES, split_axis=0,...  12.6 us
    pallas_call x1, Pallas kernels, project(): pl.pallas_call(functools.partial(project_kernel, cap), out_shape=[jax.Sha...  2.47 us
    pallas_call x1, Pallas kernels, diffuse(): pl.pallas_call(functools.partial(diffuse_kernel, ROW_BLOCK, cap), out_sha...  2.09 us
    pallas_call x1, Pallas kernels, pick(): pl.pallas_call(pick_kernel, out_shape=jax.ShapeDtypeStruct((cells, width)...  1.02 us
    pallas_call x1, Pallas kernels, project_own(): pl.pallas_call(functools.partial(project_own_kernel, cap), out_shape=[jax...  0.81 us
  transfers between devices with their start and end apart: 1, of which 1 were waited for; matrix products, arithmetic and copies ran while one was open for 0% of the time, Pallas kernels for 2%

profile of v5, /device:TPU:0, one launch (start us, length us, event | category | flops | bytes accessed | tf_op | source)
XLA Modules:
  0.0 38.4 jit_solution(12812805467695765790)
XLA Ops:
  0.0 0.0 copy-start.1
  0.0 0.0 copy-start
  0.0 0.0 copy-start.2
  0.0 2.5 %project.1 = (bf16[512,2048]{1,0:T(8,128)(2,1)S(1)}, bf16[2048,128]{1,0:T(8,128)(2,1)S(1)}, bf16[512,512]{1,0:T(8,128)(2,1)S(1)}, s32[8,512]{1,0:T(8,128)S(1)}, f32[512,128]{1,0:T(8,128)S(1)}) custom-call(bf16[1024,2048]{1,0:T(8,128)(2,1)} %x_ref.1, bf16[2048,128]{1,0:T(8,128)(2,1)} %loading_ref.1, s32[1,512]{1,0:T(1,128)} %bitcast.6, s32[1,512]{1,0:T(1,128)} %bitcast.8), custom_call_target="tpu_custom_call" | custom-call | tf_op jit(solution)/shard_map/project/pallas_call | solution.py:94
  2.5 0.6 %collective-permute-start = (f32[512,128]{1,0:T(8,128)S(1)}, f32[512,128]{1,0:T(8,128)S(1)}, u32[]{:S(2)}, u32[]{:S(2)}) collective-permute-start(f32[512,128]{1,0:T(8,128)S(1)} %get-tuple-element.23), channel_id=1, source_target_pairs={{0,1},{1,0},{2,3},{3,2},{4,5},{5,4},{6,7},{7,6},{8,9},{9,8},{10,11... | collective-permute-start | bytes 786440 | tf_op jit(solution)/shard_map/ppermute | solution.py:338
  3.1 0.0 copy-done.2
  3.1 0.0 copy-done.1
  3.1 0.0 copy-done
  3.1 0.8 %project_own.1 = (f32[512,128]{1,0:T(8,128)S(1)}, f32[32,128]{1,0:T(8,128)S(1)}, bf16[512,512]{1,0:T(8,128)(2,1)S(1)}, s32[512,128]{1,0:T(8,128)S(1)}) custom-call(bf16[512,2048]{1,0:T(8,128)(2,1)S(1)} %get-tuple-element.16.x_ref, bf16[2048,128]{1,0:T(8,128)(2,1)S(1)} %get-tuple-element.17.weights_ref, s32[1,512]{1,0:T(1,128)S(1)} %bitcast.7, ...), custom_call_target="tpu_custom_call" | custom-call | flops 268435456 | bytes 2621440 | tf_op jit(solution)/shard_map/project_own/pallas_call | solution.py:140
  3.9 0.3 collective-permute-done.refs_0_
  4.2 0.4 pack.1
  4.6 18.1 %all_to_all.10.arrived_ref = bf16[32,17,2,128]{3,2,1,0:T(2,128)(2,1)S(1)} all-to-all(bf16[32,17,2,128]{3,2,1,0:T(2,128)(2,1)S(1)} %get-tuple-element.25), channel_id=1, replica_groups=mesh['cells'=16,'genes'=2] {'cells','genes'}, dimensions={0} | all-to-all | bytes 557056 | tf_op jit(solution)/shard_map/all_to_all | solution.py:344
  22.7 2.1 %diffuse.1 = bf16[1024,128]{1,0:T(8,128)(2,1)S(1)} custom-call(bf16[32,17,2,128]{3,2,1,0:T(2,128)(2,1)S(1)} %all_to_all.10.arrived_ref), custom_call_target="tpu_custom_call" | custom-call | tf_op jit(solution)/shard_map/diffuse/pallas_call | solution.py:277
  24.8 12.6 %all_to_all.11 = bf16[32,32,128]{2,1,0:T(8,128)(2,1)S(1)} all-to-all(bf16[32,32,128]{2,1,0:T(8,128)(2,1)S(1)} %bitcast.4), channel_id=1, replica_groups=mesh['cells'=16,'genes'=2] {'cells','genes'}, dimensions={0} | all-to-all | bytes 524288 | tf_op jit(solution)/shard_map/all_to_all | solution.py:346
  37.4 1.0 %pick.1 = f32[512,128]{1,0:T(8,128)} custom-call(bf16[512,512]{1,0:T(8,128)(2,1)S(1)} %get-tuple-element.19.pick_ref, s32[512,128]{1,0:T(8,128)S(1)} %get-tuple-element.20.side_ref, bf16[1024,128]{1,0:T(8,128)(2,1)S(1)} %bitcast.5, bf16[512,128]{1,0:T(8,128)(2,1)S(1)} %get-tuple-element.26.embedded_ref), custom_call_target="tpu_custom_call" | custom-call | tf_op jit(solution)/shard_map/pick/pallas_call | solution.py:313
  (1 shorter events, 0.0 us)
Async XLA Ops:
  0.0 3.1 %copy-start.1 = (s32[512]{0:T(512)S(1)}, s32[512]{0:T(512)}, u32[]{:S(2)}) copy-start(s32[512]{0:T(512)} %param.9) | copy-start | bytes 6148
  0.0 3.1 %copy-start = (s32[512,1]{0,1:T(1,128)S(1)}, s32[512,1]{0,1:T(1,128)}, u32[]{:S(2)}) copy-start(s32[512,1]{0,1:T(1,128)} %param.8) | copy-start | bytes 6148
  0.0 3.1 %copy-start.2 = (bf16[512]{0:T(512)(128)(2,1)S(1)}, bf16[512]{0:T(512)(128)(2,1)}, u32[]{:S(2)}) copy-start(bf16[512]{0:T(512)(128)(2,1)} %param.7) | copy-start | bytes 3076
  2.5 1.7 %collective-permute-start = (f32[512,128]{1,0:T(8,128)S(1)}, f32[512,128]{1,0:T(8,128)S(1)}, u32[]{:S(2)}, u32[]{:S(2)}) collective-permute-start(f32[512,128]{1,0:T(8,128)S(1)} %get-tuple-element.23), channel_id=1, source_target_pairs={{0,1},{1,0},{2,3},{3,2},{4,5},{5,4},{6,7},{7,6},{8,9},{9,8},{10,11... | collective-permute-start | bytes 786440 | tf_op jit(solution)/shard_map/ppermute | solution.py:338
